TPU v7x, 32 devices: a whole 2x2x4 slice. The times are simulated.
32 devices in a mesh: tm: 4 (over z), space: 8 (over y, x, core).
Axes of the slice: x: 2, y: 2, z: 4, core: 2. Of those that a mesh axis runs over, the one named last changes fastest.
Arguments:
- wind: float32 [2, 4, 64, 512], P(None, 'tm', 'space'), may hold values from -0.3 to 0.3
- decay: float32 [4, 3, 64, 512], P('tm', None, 'space'), may hold values from 0.5 to 0.98
- inverse_error_variance: float32 [4, 3, 64, 512], P('tm', None, 'space'), may hold values from 0.5 to 2
- obs_index: int32 [4, 32768], P('tm', 'space'), may hold values from 0 to 12287
- obs_weight: float32 [4, 32768], P('tm', 'space'), may hold values from 0.5 to 4
- innovations: float32 [4, 32768], P('tm', 'space'), may hold values from -6 to 6
Outputs:
- increment: float32 [4, 3, 64, 512], P('tm', None, 'space')
- residual: float32 [4, 3, 64, 512], P('tm', None, 'space')
Inputs may be any that keep to these rules, and one draw needn't show every extreme that they name: `obs_index`: each observation names a flattened (field, row, column) cell of the tile of the same subwindow and tile that holds the observation; several observations may name one cell.
All inputs are finite; a program needn't handle non-finite values.
Results may differ from a plain program's by a relative error of at most 0.0001.
Values sent between devices are 32-bit elements; how exact they have to be, the bound alone decides.
A program may use at most 64 MiB of HBM per device.

v0:
```python
import jax
import jax.numpy as jnp
from jax import lax
from jax.sharding import PartitionSpec as P

STEPS = 4
ITERS = 2


diffusion = 0.15


def with_halo(block, sides, width):
    for axis, dim in sides:
        count = lax.axis_size(axis)
        forward = [(i, i + 1) for i in range(count - 1)]
        backward = [(target, source) for source, target in forward]
        low = lax.ppermute(
            lax.slice_in_dim(block, block.shape[dim] - width, None, axis=dim), axis, forward
        )
        high = lax.ppermute(lax.slice_in_dim(block, 0, width, axis=dim), axis, backward)
        block = jnp.concatenate([low, block, high], axis=dim)
    return block


def passed_along(block, axis, distance):
    devices = range(lax.axis_size(axis))
    route = [(i - distance, i) for i in devices if i - distance in devices]
    return lax.ppermute(block, axis, route)


def carried_in(shard, axis, combine, identity, reverse):
    size, index = (lax.axis_size(axis), lax.axis_index(axis))
    everything = jax.tree.map(lambda part: lax.all_gather(part, axis), shard)
    start = jax.tree.map(
        lambda part, zero: jnp.broadcast_to(jnp.asarray(zero, part.dtype), part.shape),
        shard,
        identity,
    )

    def hop(k, before):
        at = size - 1 - k if reverse else k
        reached = at > index if reverse else at < index
        new = combine(before, jax.tree.map(lambda part: part[at], everything))
        return jax.tree.map(lambda a, b: jnp.where(reached, a, b), new, before)

    return lax.fori_loop(0, size, hop, start)


def along_cols(u):
    zero_col = jnp.zeros_like(u[..., :1])
    right = jnp.concatenate([u[..., 1:], zero_col], axis=-1)
    left = jnp.concatenate([zero_col, u[..., :-1]], axis=-1)
    return (right, left)


def combine(earlier, later):
    return (earlier[0] * later[0], later[0] * earlier[1] + later[1])


def inner_product(residual, precond):
    return lax.psum(jnp.sum(residual * precond), ("tm", "space"))


def on_device(wind, decay, inverse_error_variance, obs_index, obs_weight, innovations):
    eastward_velocity = wind[0, 0]
    northward_velocity = wind[1, 0]
    shape = decay.shape
    cells = shape[1] * shape[2] * shape[3]
    index = obs_index[0]
    weight = obs_weight[0]

    def scatter_obs(values):
        return jax.ops.segment_sum(values, index, num_segments=cells).reshape(shape)

    def precondition(r):
        ident = (jnp.ones_like(r), jnp.zeros_like(r))
        later_part = carried_in((decay, r), "tm", combine, ident, True)[1]
        v_field = r + decay * later_part
        earlier_part = carried_in((decay, decay * v_field), "tm", combine, ident, False)[1]
        return v_field + earlier_part

    increment = jnp.zeros(shape, jnp.float32)
    residual = scatter_obs(weight * innovations[0])
    precond = precondition(residual)
    direction = precond
    rz_now = inner_product(residual, precond)
    for it in range(ITERS):
        tl_u = direction[0]
        for tl_step in range(STEPS):
            tl_padded = with_halo(tl_u, (("space", 1),), 1)
            tl_upper = tl_padded[:, 2:]
            tl_lower = tl_padded[:, :-2]
            tl_right, tl_left = along_cols(tl_u)
            tl_laplace = tl_upper + tl_lower + tl_right + tl_left - 4.0 * tl_u
            tl_u = (
                tl_u
                + diffusion * tl_laplace
                - 0.5 * eastward_velocity * (tl_upper - tl_lower)
                - 0.5 * northward_velocity * (tl_right - tl_left)
            )
        displaced_grid_values = passed_along(tl_u[None], "tm", 1)
        mismatch = inverse_error_variance * (direction - displaced_grid_values)
        back = passed_along(mismatch, "tm", -1)[0]
        adjoint_v = back
        for step in range(STEPS):
            stacked = jnp.stack([adjoint_v, eastward_velocity * adjoint_v])
            padded = with_halo(stacked, (("space", 2),), 1)
            padded_v = padded[0]
            padded_w = padded[1]
            upper = padded_v[:, 2:]
            lower = padded_v[:, :-2]
            right, left = along_cols(adjoint_v)
            laplace = upper + lower + right + left - 4.0 * adjoint_v
            right_z, left_solution = along_cols(northward_velocity * adjoint_v)
            adjoint_v = (
                adjoint_v
                + diffusion * laplace
                + 0.5 * (padded_w[:, 2:] - padded_w[:, :-2])
                + 0.5 * (right_z - left_solution)
            )
        back = adjoint_v
        picked = direction.reshape(cells)[index]
        image = mismatch - back[None] + scatter_obs(weight * picked)
        alpha = rz_now / lax.psum(jnp.sum(direction * image), ("tm", "space"))
        increment = increment + alpha * direction
        residual = residual - alpha * image
        if it + 1 < ITERS:
            precond = precondition(residual)
            upcoming_residual_dot = inner_product(residual, precond)
            direction = precond + upcoming_residual_dot / rz_now * direction
            rz_now = upcoming_residual_dot
    return (increment, residual)


def solution(mesh):
    placed = (
        P(None, "tm", "space", None),
        P("tm", None, "space", None),
        P("tm", None, "space", None),
        P("tm", "space"),
        P("tm", "space"),
        P("tm", "space"),
    )
    return jax.shard_map(
        on_device,
        mesh=mesh,
        in_specs=placed,
        out_specs=(P("tm", None, "space", None), P("tm", None, "space", None)),
        check_vma=False,
    )
```

profile of v0, /device:TPU:0, one launch (start us, length us, event | category | flops | bytes accessed | tf_op | source)
XLA Modules:
  0.0 459.1 jit_solution(14174619644742302327)
XLA Ops:
  0.7 0.7 mul.475
  1.4 21.9 %scatter_custom_fusion = f32[12288]{0:T(1024)S(1)} fusion(s32[4096]{0:T(1024)S(1)} %bitcast.189, f32[4096]{0:T(1024)S(1)} %mul.475, f32[]{:T(128)} %constant.143.clone.1), kind=kCustom, calls=%fused_computation.184 | custom fusion | flops 4096 | bytes 49156 | tf_op jit(solution)/shard_map/scatter-add | solution.py:74
  23.4 15.6 %all_gather.35 = f32[4,1,3,8,512]{4,3,2,1,0:T(8,128)S(1)} all-gather(f32[1,1,3,8,512]{4,3,2,1,0:T(8,128)S(1)} %all_gather_reshape.3), channel_id=1, replica_groups=mesh['tm'=4,'space'=8] {'tm'}, dimensions={0}, use_global_device_ids=true | all-gather | bytes 245760 | tf_op jit(solution)/shard_map/all_gather | solution.py:34
  38.9 14.1 %all-gather = f32[4,3,8,512]{3,2,1,0:T(8,128)S(1)} all-gather(f32[1,3,8,512]{3,2,1,0:T(8,128)S(1)} %copy-done), channel_id=2, replica_groups=mesh['tm'=4,'space'=8] {'tm'}, dimensions={0}, use_global_device_ids=true | all-gather | bytes 245760 | tf_op jit(solution)/shard_map/all_gather | solution.py:34
  53.3 13.6 %all-gather.1 = f32[4,3,8,512]{3,2,1,0:T(8,128)S(1)} all-gather(f32[1,3,8,512]{3,2,1,0:T(8,128)S(1)} %fusion.81), channel_id=3, replica_groups=mesh['tm'=4,'space'=8] {'tm'}, dimensions={0}, use_global_device_ids=true | all-gather | bytes 245760 | tf_op jit(solution)/shard_map/all_gather | solution.py:34
  67.0 1.3 collective-permute-start
  68.3 3.0 collective-permute-start.1
  71.5 0.7 copy-done.3
  72.4 1.3 collective-permute-start.2
  73.7 3.6 collective-permute-start.3
  77.4 0.7 collective-permute-done.3
  78.2 1.3 collective-permute-start.4
  79.5 4.7 %collective-permute-start.5 = (f32[3,1,512]{2,1,0:T(1,128)S(1)}, f32[3,1,512]{2,1,0:T(1,128)S(1)}, u32[]{:S(2)}, u32[]{:S(2)}) collective-permute-start(f32[3,1,512]{2,1,0:T(1,128)S(1)} %get-tuple-element.723), channel_id=1, source_target_pairs={{0,1},{1,2},{2,3},{3,4},{4,5},{5,6},{6,7},{8,9},{9,10},{10,11},{11... | collective-permute-start | bytes 18440 | tf_op jit(solution)/shard_map/ppermute | solution.py:18
  85.1 1.3 collective-permute-start.6
  86.4 4.8 %collective-permute-start.7 = (f32[3,1,512]{2,1,0:T(1,128)S(1)}, f32[3,1,512]{2,1,0:T(1,128)S(1)}, u32[]{:S(2)}, u32[]{:S(2)}) collective-permute-start(f32[3,1,512]{2,1,0:T(1,128)S(1)} %get-tuple-element.719), channel_id=1, source_target_pairs={{0,1},{1,2},{2,3},{3,4},{4,5},{5,6},{6,7},{8,9},{9,10},{10,11},{11... | collective-permute-start | bytes 18440 | tf_op jit(solution)/shard_map/ppermute | solution.py:18
  92.1 3.5 collective-permute-start.8
  95.6 1.7 collective-permute-done.8
  97.3 1.3 collective-permute-start.9
  98.7 23.0 %gather_fusion = f32[4096]{0:T(1024)S(1)} fusion(f32[12288]{0:T(1024)S(1)} %bitcast.157, s32[4096]{0:T(1024)S(1)} %broadcast_clamp_fusion), kind=kCustom, calls=%fused_computation | custom fusion | bytes 49152 | tf_op jit(solution)/shard_map/gather | solution.py:123
  121.8 21.9 %scatter_custom_fusion.1 = f32[12288]{0:T(1024)S(1)} fusion(s32[4096]{0:T(1024)S(1)} %bitcast.190, f32[4096]{0:T(1024)S(1)} %mul.527, f32[]{:T(128)} %constant.143.clone.1), kind=kCustom, calls=%fused_computation.182 | custom fusion | flops 4096 | bytes 49156 | tf_op jit(solution)/shard_map/scatter-add | solution.py:74
  143.7 3.3 collective-permute-start.10
  147.0 1.3 collective-permute-start.11
  148.5 4.2 collective-permute-done.11
  152.9 4.3 collective-permute-start.12
  157.3 1.3 collective-permute-start.13
  158.7 3.9 collective-permute-done.13
  162.9 6.0 %collective-permute-start.14 = (f32[2,3,1,512]{3,2,1,0:T(1,128)S(1)}, f32[2,3,1,512]{3,2,1,0:T(1,128)S(1)}, u32[]{:S(2)}, u32[]{:S(2)}) collective-permute-start(f32[2,3,1,512]{3,2,1,0:T(1,128)S(1)} %get-tuple-element.665), channel_id=1, source_target_pairs={{0,1},{1,2},{2,3},{3,4},{4,5},{5,6},{6,7},{8,9},{9,10},{10,11},{11... | collective-permute-start | bytes 36872 | tf_op jit(solution)/shard_map/ppermute | solution.py:18
  168.9 1.3 collective-permute-start.15
  170.3 1.7 collective-permute-done.15
  172.2 4.8 %collective-permute-start.16 = (f32[2,3,1,512]{3,2,1,0:T(1,128)S(1)}, f32[2,3,1,512]{3,2,1,0:T(1,128)S(1)}, u32[]{:S(2)}, u32[]{:S(2)}) collective-permute-start(f32[2,3,1,512]{3,2,1,0:T(1,128)S(1)} %get-tuple-element.663), channel_id=1, source_target_pairs={{0,1},{1,2},{2,3},{3,4},{4,5},{5,6},{6,7},{8,9},{9,10},{10,11},{11... | collective-permute-start | bytes 36872 | tf_op jit(solution)/shard_map/ppermute | solution.py:18
  177.0 1.3 collective-permute-start.17
  178.4 1.7 collective-permute-done.17
  180.2 0.8 multiply_reduce_fusion.2
  181.0 45.0 %all-reduce.48 = (f32[]{:T(128)}, f32[]{:T(128)}) all-reduce(f32[]{:T(128)} %get-tuple-element.581, f32[]{:T(128)} %get-tuple-element.580), channel_id=1, replica_groups=mesh['tm'=4,'space'=8] {'tm','space'}, use_global_device_ids=true, to_apply=%region_6.7 | all-reduce | flops 2 | bytes 16 | tf_op jit(solution)/shard_map/psum | solution.py:62
  227.3 13.6 %all-gather.2 = f32[4,3,8,512]{3,2,1,0:T(8,128)S(1)} all-gather(f32[1,3,8,512]{3,2,1,0:T(8,128)S(1)} %multiply_subtract_fusion.4), channel_id=4, replica_groups=mesh['tm'=4,'space'=8] {'tm'}, dimensions={0}, use_global_device_ids=true | all-gather | bytes 245760 | tf_op jit(solution)/shard_map/all_gather | solution.py:34
  241.1 13.6 %all-gather.3 = f32[4,3,8,512]{3,2,1,0:T(8,128)S(1)} all-gather(f32[1,3,8,512]{3,2,1,0:T(8,128)S(1)} %fusion.83), channel_id=5, replica_groups=mesh['tm'=4,'space'=8] {'tm'}, dimensions={0}, use_global_device_ids=true | all-gather | bytes 245760 | tf_op jit(solution)/shard_map/all_gather | solution.py:34
  255.5 40.0 %psum.30 = f32[]{:T(128)} all-reduce(f32[]{:T(128)} %multiply_reduce_fusion.1), channel_id=1, replica_groups=mesh['tm'=4,'space'=8] {'tm','space'}, use_global_device_ids=true, to_apply=%region_15.16 | all-reduce | flops 1 | bytes 8 | tf_op jit(solution)/shard_map/psum | solution.py:62
  296.8 1.3 collective-permute-start.18
  298.1 3.0 collective-permute-start.19
  302.0 1.3 collective-permute-start.20
  303.3 4.4 collective-permute-start.21
  307.8 0.7 collective-permute-done.21
  308.6 1.3 collective-permute-start.22
  309.9 4.8 %collective-permute-start.23 = (f32[3,1,512]{2,1,0:T(1,128)S(1)}, f32[3,1,512]{2,1,0:T(1,128)S(1)}, u32[]{:S(2)}, u32[]{:S(2)}) collective-permute-start(f32[3,1,512]{2,1,0:T(1,128)S(1)} %get-tuple-element.691), channel_id=1, source_target_pairs={{0,1},{1,2},{2,3},{3,4},{4,5},{5,6},{6,7},{8,9},{9,10},{10,11},{11... | collective-permute-start | bytes 18440 | tf_op jit(solution)/shard_map/ppermute | solution.py:18
  315.6 1.3 collective-permute-start.24
  316.9 4.8 %collective-permute-start.25 = (f32[3,1,512]{2,1,0:T(1,128)S(1)}, f32[3,1,512]{2,1,0:T(1,128)S(1)}, u32[]{:S(2)}, u32[]{:S(2)}) collective-permute-start(f32[3,1,512]{2,1,0:T(1,128)S(1)} %get-tuple-element.687), channel_id=1, source_target_pairs={{0,1},{1,2},{2,3},{3,4},{4,5},{5,6},{6,7},{8,9},{9,10},{10,11},{11... | collective-permute-start | bytes 18440 | tf_op jit(solution)/shard_map/ppermute | solution.py:18
  322.6 3.5 collective-permute-start.26
  326.1 1.7 collective-permute-done.26
  327.9 1.3 collective-permute-start.27
  329.2 23.0 %gather_fusion.1 = f32[4096]{0:T(1024)S(1)} fusion(f32[12288]{0:T(1024)S(1)} %bitcast.156, s32[4096]{0:T(1024)S(1)} %broadcast_clamp_fusion), kind=kCustom, calls=%fused_computation.1 | custom fusion | bytes 49152 | tf_op jit(solution)/shard_map/gather | solution.py:123
  352.2 21.9 %scatter_custom_fusion.2 = f32[12288]{0:T(1024)S(1)} fusion(s32[4096]{0:T(1024)S(1)} %bitcast.191, f32[4096]{0:T(1024)S(1)} %mul.578, f32[]{:T(128)} %constant.143.clone.1), kind=kCustom, calls=%fused_computation.180 | custom fusion | flops 4096 | bytes 49156 | tf_op jit(solution)/shard_map/scatter-add | solution.py:74
  374.2 3.3 collective-permute-start.28
  377.5 1.3 collective-permute-start.29
  379.0 4.2 collective-permute-done.29
  383.5 4.3 collective-permute-start.30
  387.9 1.3 collective-permute-start.31
  389.3 4.1 collective-permute-done.31
  393.7 6.0 %collective-permute-start.32 = (f32[2,3,1,512]{3,2,1,0:T(1,128)S(1)}, f32[2,3,1,512]{3,2,1,0:T(1,128)S(1)}, u32[]{:S(2)}, u32[]{:S(2)}) collective-permute-start(f32[2,3,1,512]{3,2,1,0:T(1,128)S(1)} %get-tuple-element.657), channel_id=1, source_target_pairs={{0,1},{1,2},{2,3},{3,4},{4,5},{5,6},{6,7},{8,9},{9,10},{10,11},{11... | collective-permute-start | bytes 36872 | tf_op jit(solution)/shard_map/ppermute | solution.py:18
  399.6 1.3 collective-permute-start.33
  401.0 1.7 collective-permute-done.33
  403.0 4.8 %collective-permute-start.34 = (f32[2,3,1,512]{3,2,1,0:T(1,128)S(1)}, f32[2,3,1,512]{3,2,1,0:T(1,128)S(1)}, u32[]{:S(2)}, u32[]{:S(2)}) collective-permute-start(f32[2,3,1,512]{3,2,1,0:T(1,128)S(1)} %get-tuple-element.655), channel_id=1, source_target_pairs={{0,1},{1,2},{2,3},{3,4},{4,5},{5,6},{6,7},{8,9},{9,10},{10,11},{11... | collective-permute-start | bytes 36872 | tf_op jit(solution)/shard_map/ppermute | solution.py:18
  407.8 1.3 collective-permute-start.35
  409.2 1.7 collective-permute-done.35
  411.6 44.9 %psum.31 = f32[]{:T(128)} all-reduce(f32[]{:T(128)} %get-tuple-element.624), channel_id=1, replica_groups=mesh['tm'=4,'space'=8] {'tm','space'}, use_global_device_ids=true, to_apply=%region_18.19 | all-reduce | flops 1 | bytes 8 | tf_op jit(solution)/shard_map/psum | solution.py:125
  (159 shorter events, 11.3 us)
Async XLA Ops:
  0.6 0.8 copy-start.4
  23.3 15.6 %copy-start = (f32[1,3,8,512]{3,2,1,0:T(8,128)S(1)}, f32[1,3,8,512]{3,2,1,0:T(8,128)}, u32[]{:S(2)}) copy-start(f32[1,3,8,512]{3,2,1,0:T(8,128)} %param.15) | copy-start | bytes 147460
  67.0 5.2 %collective-permute-start = (f32[3,1,512]{2,1,0:T(1,128)S(1)}, f32[3,1,512]{2,1,0:T(1,128)S(1)}, u32[]{:S(2)}, u32[]{:S(2)}) collective-permute-start(f32[3,1,512]{2,1,0:T(1,128)S(1)} %get-tuple-element.732), channel_id=1, source_target_pairs={{1,0},{2,1},{3,2},{4,3},{5,4},{6,5},{7,6},{9,8},{10,9},{11,10},{12... | collective-permute-start | bytes 18440 | tf_op jit(solution)/shard_map/ppermute | solution.py:21
  68.3 3.9 collective-permute-start.1
  71.5 0.8 copy-start.3
  72.4 5.0 %collective-permute-start.2 = (f32[3,1,512]{2,1,0:T(1,128)S(1)}, f32[3,1,512]{2,1,0:T(1,128)S(1)}, u32[]{:S(2)}, u32[]{:S(2)}) collective-permute-start(f32[3,1,512]{2,1,0:T(1,128)S(1)} %get-tuple-element.728), channel_id=1, source_target_pairs={{1,0},{2,1},{3,2},{4,3},{5,4},{6,5},{7,6},{9,8},{10,9},{11,10},{12... | collective-permute-start | bytes 18440 | tf_op jit(solution)/shard_map/ppermute | solution.py:21
  73.7 4.5 collective-permute-start.3
  78.2 6.0 %collective-permute-start.4 = (f32[3,1,512]{2,1,0:T(1,128)S(1)}, f32[3,1,512]{2,1,0:T(1,128)S(1)}, u32[]{:S(2)}, u32[]{:S(2)}) collective-permute-start(f32[3,1,512]{2,1,0:T(1,128)S(1)} %get-tuple-element.724), channel_id=1, source_target_pairs={{1,0},{2,1},{3,2},{4,3},{5,4},{6,5},{7,6},{9,8},{10,9},{11,10},{12... | collective-permute-start | bytes 18440 | tf_op jit(solution)/shard_map/ppermute | solution.py:21
  79.5 5.5 %collective-permute-start.5 = (f32[3,1,512]{2,1,0:T(1,128)S(1)}, f32[3,1,512]{2,1,0:T(1,128)S(1)}, u32[]{:S(2)}, u32[]{:S(2)}) collective-permute-start(f32[3,1,512]{2,1,0:T(1,128)S(1)} %get-tuple-element.723), channel_id=1, source_target_pairs={{0,1},{1,2},{2,3},{3,4},{4,5},{5,6},{6,7},{8,9},{9,10},{10,11},{11... | collective-permute-start | bytes 18440 | tf_op jit(solution)/shard_map/ppermute | solution.py:18
  85.1 6.1 %collective-permute-start.6 = (f32[3,1,512]{2,1,0:T(1,128)S(1)}, f32[3,1,512]{2,1,0:T(1,128)S(1)}, u32[]{:S(2)}, u32[]{:S(2)}) collective-permute-start(f32[3,1,512]{2,1,0:T(1,128)S(1)} %get-tuple-element.720), channel_id=1, source_target_pairs={{1,0},{2,1},{3,2},{4,3},{5,4},{6,5},{7,6},{9,8},{10,9},{11,10},{12... | collective-permute-start | bytes 18440 | tf_op jit(solution)/shard_map/ppermute | solution.py:21
  86.4 5.6 %collective-permute-start.7 = (f32[3,1,512]{2,1,0:T(1,128)S(1)}, f32[3,1,512]{2,1,0:T(1,128)S(1)}, u32[]{:S(2)}, u32[]{:S(2)}) collective-permute-start(f32[3,1,512]{2,1,0:T(1,128)S(1)} %get-tuple-element.719), channel_id=1, source_target_pairs={{0,1},{1,2},{2,3},{3,4},{4,5},{5,6},{6,7},{8,9},{9,10},{10,11},{11... | collective-permute-start | bytes 18440 | tf_op jit(solution)/shard_map/ppermute | solution.py:18
  92.1 5.2 %copy-start.1 = (f32[1,3,8,512]{3,2,1,0:T(8,128)S(1)}, f32[1,3,8,512]{3,2,1,0:T(8,128)}, u32[]{:S(2)}) copy-start(f32[1,3,8,512]{3,2,1,0:T(8,128)} %param.16) | copy-start | bytes 147460
  92.1 5.2 %collective-permute-start.8 = (f32[1,3,8,512]{3,2,1,0:T(8,128)S(1)}, f32[1,3,8,512]{3,2,1,0:T(8,128)S(1)}, u32[]{:S(2)}, u32[]{:S(2)}) collective-permute-start(f32[1,3,8,512]{3,2,1,0:T(8,128)S(1)} %subtract_bitcast_fusion.1), channel_id=1, source_target_pairs={{0,8},{8,16},{16,24},{1,9},{9,17},{17,25},{2,10},{10,18},{18,26},{... | collective-permute-start | bytes 147464 | tf_op jit(solution)/shard_map/ppermute | solution.py:29
  97.3 46.4 %collective-permute-start.9 = (f32[1,3,8,512]{3,2,1,0:T(8,128)S(1)}, f32[1,3,8,512]{3,2,1,0:T(8,128)S(1)}, u32[]{:S(2)}, u32[]{:S(2)}) collective-permute-start(f32[1,3,8,512]{3,2,1,0:T(8,128)S(1)} %subtract_multiply_fusion.1), channel_id=1, source_target_pairs={{8,0},{16,8},{24,16},{9,1},{17,9},{25,17},{10,2},{18,10},{26,18},{... | collective-permute-start | bytes 147464 | tf_op jit(solution)/shard_map/ppermute | solution.py:29
  98.7 23.1 %copy-start.2 = (f32[1,4096]{1,0:T(1,128)S(1)}, f32[1,4096]{1,0:T(1,128)}, u32[]{:S(2)}) copy-start(f32[1,4096]{1,0:T(1,128)} %param.18) | copy-start | bytes 49156
  143.7 4.8 %collective-permute-start.10 = (f32[2,3,1,512]{3,2,1,0:T(1,128)S(1)}, f32[2,3,1,512]{3,2,1,0:T(1,128)S(1)}, u32[]{:S(2)}, u32[]{:S(2)}) collective-permute-start(f32[2,3,1,512]{3,2,1,0:T(1,128)S(1)} %get-tuple-element.669), channel_id=1, source_target_pairs={{0,1},{1,2},{2,3},{3,4},{4,5},{5,6},{6,7},{8,9},{9,10},{10,11},{11... | collective-permute-start | bytes 36872 | tf_op jit(solution)/shard_map/ppermute | solution.py:18
  147.0 5.7 %collective-permute-start.11 = (f32[2,3,1,512]{3,2,1,0:T(1,128)S(1)}, f32[2,3,1,512]{3,2,1,0:T(1,128)S(1)}, u32[]{:S(2)}, u32[]{:S(2)}) collective-permute-start(f32[2,3,1,512]{3,2,1,0:T(1,128)S(1)} %get-tuple-element.670), channel_id=1, source_target_pairs={{1,0},{2,1},{3,2},{4,3},{5,4},{6,5},{7,6},{9,8},{10,9},{11,10},{12... | collective-permute-start | bytes 36872 | tf_op jit(solution)/shard_map/ppermute | solution.py:21
  152.9 5.7 %collective-permute-start.12 = (f32[2,3,1,512]{3,2,1,0:T(1,128)S(1)}, f32[2,3,1,512]{3,2,1,0:T(1,128)S(1)}, u32[]{:S(2)}, u32[]{:S(2)}) collective-permute-start(f32[2,3,1,512]{3,2,1,0:T(1,128)S(1)} %get-tuple-element.667), channel_id=1, source_target_pairs={{0,1},{1,2},{2,3},{3,4},{4,5},{5,6},{6,7},{8,9},{9,10},{10,11},{11... | collective-permute-start | bytes 36872 | tf_op jit(solution)/shard_map/ppermute | solution.py:18
  157.3 5.3 %collective-permute-start.13 = (f32[2,3,1,512]{3,2,1,0:T(1,128)S(1)}, f32[2,3,1,512]{3,2,1,0:T(1,128)S(1)}, u32[]{:S(2)}, u32[]{:S(2)}) collective-permute-start(f32[2,3,1,512]{3,2,1,0:T(1,128)S(1)} %get-tuple-element.668), channel_id=1, source_target_pairs={{1,0},{2,1},{3,2},{4,3},{5,4},{6,5},{7,6},{9,8},{10,9},{11,10},{12... | collective-permute-start | bytes 36872 | tf_op jit(solution)/shard_map/ppermute | solution.py:21
  162.9 7.3 %collective-permute-start.14 = (f32[2,3,1,512]{3,2,1,0:T(1,128)S(1)}, f32[2,3,1,512]{3,2,1,0:T(1,128)S(1)}, u32[]{:S(2)}, u32[]{:S(2)}) collective-permute-start(f32[2,3,1,512]{3,2,1,0:T(1,128)S(1)} %get-tuple-element.665), channel_id=1, source_target_pairs={{0,1},{1,2},{2,3},{3,4},{4,5},{5,6},{6,7},{8,9},{9,10},{10,11},{11... | collective-permute-start | bytes 36872 | tf_op jit(solution)/shard_map/ppermute | solution.py:18
  168.9 3.1 collective-permute-start.15
  172.2 6.2 %collective-permute-start.16 = (f32[2,3,1,512]{3,2,1,0:T(1,128)S(1)}, f32[2,3,1,512]{3,2,1,0:T(1,128)S(1)}, u32[]{:S(2)}, u32[]{:S(2)}) collective-permute-start(f32[2,3,1,512]{3,2,1,0:T(1,128)S(1)} %get-tuple-element.663), channel_id=1, source_target_pairs={{0,1},{1,2},{2,3},{3,4},{4,5},{5,6},{6,7},{8,9},{9,10},{10,11},{11... | collective-permute-start | bytes 36872 | tf_op jit(solution)/shard_map/ppermute | solution.py:18
  177.0 3.1 collective-permute-start.17
  296.8 4.4 collective-permute-start.18
  298.1 3.8 collective-permute-start.19
  302.0 5.8 %collective-permute-start.20 = (f32[3,1,512]{2,1,0:T(1,128)S(1)}, f32[3,1,512]{2,1,0:T(1,128)S(1)}, u32[]{:S(2)}, u32[]{:S(2)}) collective-permute-start(f32[3,1,512]{2,1,0:T(1,128)S(1)} %get-tuple-element.696), channel_id=1, source_target_pairs={{1,0},{2,1},{3,2},{4,3},{5,4},{6,5},{7,6},{9,8},{10,9},{11,10},{12... | collective-permute-start | bytes 18440 | tf_op jit(solution)/shard_map/ppermute | solution.py:21
  303.3 5.2 %collective-permute-start.21 = (f32[3,1,512]{2,1,0:T(1,128)S(1)}, f32[3,1,512]{2,1,0:T(1,128)S(1)}, u32[]{:S(2)}, u32[]{:S(2)}) collective-permute-start(f32[3,1,512]{2,1,0:T(1,128)S(1)} %get-tuple-element.695), channel_id=1, source_target_pairs={{0,1},{1,2},{2,3},{3,4},{4,5},{5,6},{6,7},{8,9},{9,10},{10,11},{11... | collective-permute-start | bytes 18440 | tf_op jit(solution)/shard_map/ppermute | solution.py:18
  308.6 6.1 %collective-permute-start.22 = (f32[3,1,512]{2,1,0:T(1,128)S(1)}, f32[3,1,512]{2,1,0:T(1,128)S(1)}, u32[]{:S(2)}, u32[]{:S(2)}) collective-permute-start(f32[3,1,512]{2,1,0:T(1,128)S(1)} %get-tuple-element.692), channel_id=1, source_target_pairs={{1,0},{2,1},{3,2},{4,3},{5,4},{6,5},{7,6},{9,8},{10,9},{11,10},{12... | collective-permute-start | bytes 18440 | tf_op jit(solution)/shard_map/ppermute | solution.py:21
  309.9 5.6 %collective-permute-start.23 = (f32[3,1,512]{2,1,0:T(1,128)S(1)}, f32[3,1,512]{2,1,0:T(1,128)S(1)}, u32[]{:S(2)}, u32[]{:S(2)}) collective-permute-start(f32[3,1,512]{2,1,0:T(1,128)S(1)} %get-tuple-element.691), channel_id=1, source_target_pairs={{0,1},{1,2},{2,3},{3,4},{4,5},{5,6},{6,7},{8,9},{9,10},{10,11},{11... | collective-permute-start | bytes 18440 | tf_op jit(solution)/shard_map/ppermute | solution.py:18
  315.6 6.1 %collective-permute-start.24 = (f32[3,1,512]{2,1,0:T(1,128)S(1)}, f32[3,1,512]{2,1,0:T(1,128)S(1)}, u32[]{:S(2)}, u32[]{:S(2)}) collective-permute-start(f32[3,1,512]{2,1,0:T(1,128)S(1)} %get-tuple-element.688), channel_id=1, source_target_pairs={{1,0},{2,1},{3,2},{4,3},{5,4},{6,5},{7,6},{9,8},{10,9},{11,10},{12... | collective-permute-start | bytes 18440 | tf_op jit(solution)/shard_map/ppermute | solution.py:21
  316.9 5.6 %collective-permute-start.25 = (f32[3,1,512]{2,1,0:T(1,128)S(1)}, f32[3,1,512]{2,1,0:T(1,128)S(1)}, u32[]{:S(2)}, u32[]{:S(2)}) collective-permute-start(f32[3,1,512]{2,1,0:T(1,128)S(1)} %get-tuple-element.687), channel_id=1, source_target_pairs={{0,1},{1,2},{2,3},{3,4},{4,5},{5,6},{6,7},{8,9},{9,10},{10,11},{11... | collective-permute-start | bytes 18440 | tf_op jit(solution)/shard_map/ppermute | solution.py:18
  322.6 5.3 %collective-permute-start.26 = (f32[1,3,8,512]{3,2,1,0:T(8,128)S(1)}, f32[1,3,8,512]{3,2,1,0:T(8,128)S(1)}, u32[]{:S(2)}, u32[]{:S(2)}) collective-permute-start(f32[1,3,8,512]{3,2,1,0:T(8,128)S(1)} %subtract_bitcast_fusion), channel_id=1, source_target_pairs={{0,8},{8,16},{16,24},{1,9},{9,17},{17,25},{2,10},{10,18},{18,26},{... | collective-permute-start | bytes 147464 | tf_op jit(solution)/shard_map/ppermute | solution.py:29
  327.9 46.3 %collective-permute-start.27 = (f32[1,3,8,512]{3,2,1,0:T(8,128)S(1)}, f32[1,3,8,512]{3,2,1,0:T(8,128)S(1)}, u32[]{:S(2)}, u32[]{:S(2)}) collective-permute-start(f32[1,3,8,512]{3,2,1,0:T(8,128)S(1)} %subtract_multiply_fusion), channel_id=1, source_target_pairs={{8,0},{16,8},{24,16},{9,1},{17,9},{25,17},{10,2},{18,10},{26,18},{... | collective-permute-start | bytes 147464 | tf_op jit(solution)/shard_map/ppermute | solution.py:29
  374.2 4.8 %collective-permute-start.28 = (f32[2,3,1,512]{3,2,1,0:T(1,128)S(1)}, f32[2,3,1,512]{3,2,1,0:T(1,128)S(1)}, u32[]{:S(2)}, u32[]{:S(2)}) collective-permute-start(f32[2,3,1,512]{3,2,1,0:T(1,128)S(1)} %get-tuple-element.661), channel_id=1, source_target_pairs={{0,1},{1,2},{2,3},{3,4},{4,5},{5,6},{6,7},{8,9},{9,10},{10,11},{11... | collective-permute-start | bytes 36872 | tf_op jit(solution)/shard_map/ppermute | solution.py:18
  377.5 5.7 %collective-permute-start.29 = (f32[2,3,1,512]{3,2,1,0:T(1,128)S(1)}, f32[2,3,1,512]{3,2,1,0:T(1,128)S(1)}, u32[]{:S(2)}, u32[]{:S(2)}) collective-permute-start(f32[2,3,1,512]{3,2,1,0:T(1,128)S(1)} %get-tuple-element.662), channel_id=1, source_target_pairs={{1,0},{2,1},{3,2},{4,3},{5,4},{6,5},{7,6},{9,8},{10,9},{11,10},{12... | collective-permute-start | bytes 36872 | tf_op jit(solution)/shard_map/ppermute | solution.py:21
  383.5 5.7 %collective-permute-start.30 = (f32[2,3,1,512]{3,2,1,0:T(1,128)S(1)}, f32[2,3,1,512]{3,2,1,0:T(1,128)S(1)}, u32[]{:S(2)}, u32[]{:S(2)}) collective-permute-start(f32[2,3,1,512]{3,2,1,0:T(1,128)S(1)} %get-tuple-element.659), channel_id=1, source_target_pairs={{0,1},{1,2},{2,3},{3,4},{4,5},{5,6},{6,7},{8,9},{9,10},{10,11},{11... | collective-permute-start | bytes 36872 | tf_op jit(solution)/shard_map/ppermute | solution.py:18
  387.9 5.5 %collective-permute-start.31 = (f32[2,3,1,512]{3,2,1,0:T(1,128)S(1)}, f32[2,3,1,512]{3,2,1,0:T(1,128)S(1)}, u32[]{:S(2)}, u32[]{:S(2)}) collective-permute-start(f32[2,3,1,512]{3,2,1,0:T(1,128)S(1)} %get-tuple-element.660), channel_id=1, source_target_pairs={{1,0},{2,1},{3,2},{4,3},{5,4},{6,5},{7,6},{9,8},{10,9},{11,10},{12... | collective-permute-start | bytes 36872 | tf_op jit(solution)/shard_map/ppermute | solution.py:21
  393.7 7.3 %collective-permute-start.32 = (f32[2,3,1,512]{3,2,1,0:T(1,128)S(1)}, f32[2,3,1,512]{3,2,1,0:T(1,128)S(1)}, u32[]{:S(2)}, u32[]{:S(2)}) collective-permute-start(f32[2,3,1,512]{3,2,1,0:T(1,128)S(1)} %get-tuple-element.657), channel_id=1, source_target_pairs={{0,1},{1,2},{2,3},{3,4},{4,5},{5,6},{6,7},{8,9},{9,10},{10,11},{11... | collective-permute-start | bytes 36872 | tf_op jit(solution)/shard_map/ppermute | solution.py:18
  399.6 3.1 collective-permute-start.33
  403.0 6.2 %collective-permute-start.34 = (f32[2,3,1,512]{3,2,1,0:T(1,128)S(1)}, f32[2,3,1,512]{3,2,1,0:T(1,128)S(1)}, u32[]{:S(2)}, u32[]{:S(2)}) collective-permute-start(f32[2,3,1,512]{3,2,1,0:T(1,128)S(1)} %get-tuple-element.655), channel_id=1, source_target_pairs={{0,1},{1,2},{2,3},{3,4},{4,5},{5,6},{6,7},{8,9},{9,10},{10,11},{11... | collective-permute-start | bytes 36872 | tf_op jit(solution)/shard_map/ppermute | solution.py:18
  407.8 3.1 collective-permute-start.35
where the time goes:
time: 461 us; the launch traced here: 459 us
  blocking collectives  200 us (43%)
  starting transfers between devices  100 us (22%)
  other arithmetic  72.1 us (16%)
  local copies, waits for them, and re-layouts  48.9 us (11%)
  waiting for transfers between devices  31.9 us (7%)
  between operations  5.55 us (1%)
    psum x2, blocking collectives, inner_product(): return lax.psum(jnp.sum(residual * precond), ('tm', 'space'))  85 us
    all_gather x5, blocking collectives, carried_in(): everything = jax.tree.map(lambda part: lax.all_gather(part, axis), shard)  70.5 us
    ppermute x16, starting transfers between devices, with_halo(): lax.ppermute(lax.slice_in_dim(block, block.shape[dim] - width, None, axis...  69.7 us
    scatter-add x3, other arithmetic, scatter_obs(): return jax.ops.segment_sum(values, index, num_segments=cells).reshape(shape)  65.7 us
    gather x2, local copies, waits for them, and re-layouts, on_device(): picked = direction.reshape(cells)[index]  46.1 us
    psum x1, blocking collectives, on_device(): alpha = rz_now / lax.psum(jnp.sum(direction * image), ('tm', 'space'))  44.9 us
    ppermute x16, waiting for transfers between devices, with_halo(): lax.ppermute(lax.slice_in_dim(block, 0, width, axis=dim), axis, backward)  23.3 us
    ppermute x16, starting transfers between devices, with_halo(): lax.ppermute(lax.slice_in_dim(block, 0, width, axis=dim), axis, backward)  20.7 us
  transfers between devices with their start and end apart: 36, of which 17 were waited for; matrix products, arithmetic and copies ran while one was open for 20% of the time, Pallas kernels for 0%

commit v1 on v0

v1 whole, which is shorter than its diff:
```python
import functools

import jax
import jax.numpy as jnp
from jax import lax
from jax.experimental import pallas as pl
from jax.experimental.pallas import tpu as pltpu
from jax.sharding import PartitionSpec as P

STEPS = 4
DIFFUSION = 0.15
MESH = pl.DeviceIdType.MESH
CHUNK = 1024


def split3(x):
    high = x.astype(jnp.bfloat16)
    rest = x - high.astype(jnp.float32)
    mid = rest.astype(jnp.bfloat16)
    low = (rest - mid.astype(jnp.float32)).astype(jnp.bfloat16)
    return high, mid, low


def folded(x):
    rows = x[0] + x[1] + x[2]
    width = rows.shape[1]
    total = rows[:, :128]
    for at in range(128, width, 128):
        total = total + rows[:, at : at + 128]
    return total


def whole(x):
    return jnp.sum(x, axis=(0, 1), keepdims=True)


def kernel(
    n_tm, n_sp, wind, decay, iev, obs, weight, innov, inc_out, res_out,
    dec_all, r_all, q_all, z_all, y_all, wind_ext, iev_next, iev_ext, d_ext, f_send, f_recv,
    sum_tm, sum_sp, diag, tm_send, tm_recv, sp_send, sp_recv, st_send, st_recv,
):
    k = lax.axis_index("tm")
    s = lax.axis_index("space")
    fields, rows, width = decay.shape[1:]
    has_next, has_prev = k < n_tm - 1, k > 0
    has_high, has_low = s < n_sp - 1, s > 0
    pending = []

    def tm_at(o):
        return lax.rem(k + o + n_tm, n_tm)

    def sp_at(o):
        return lax.rem(s + o + n_sp, n_sp)

    barrier = pltpu.get_barrier_semaphore()
    for o in range(1, n_tm):
        pl.semaphore_signal(barrier, inc=1, device_id=(tm_at(o), s), device_id_type=MESH)
    for o in range(1, n_sp):
        pl.semaphore_signal(barrier, inc=1, device_id=(k, sp_at(o)), device_id_type=MESH)
    pl.semaphore_wait(barrier, n_tm + n_sp - 2)

    def remote(src, dst, send, recv, device):
        return pltpu.make_async_remote_copy(
            src_ref=src, dst_ref=dst, send_sem=send, recv_sem=recv,
            device_id=device, device_id_type=MESH,
        )

    def start(copy, cond=None):
        pending.append((copy, cond))
        if cond is None:
            copy.start()
        else:
            pl.when(cond)(copy.start)

    def spread_tm(buffer, use):
        for o in range(1, n_tm):
            start(remote(buffer.at[k], buffer.at[k], tm_send.at[use, o], tm_recv.at[use, o], (tm_at(o), s)))

    def arrive_tm(buffer, use):
        for o in range(1, n_tm):
            src = tm_at(-o)
            remote(buffer.at[src], buffer.at[src], tm_send.at[use, o], tm_recv.at[use, o], (src, s)).wait_recv()

    def spread_sp(buffer, use):
        for o in range(1, n_sp):
            start(remote(buffer.at[s], buffer.at[s], sp_send.at[use, o], sp_recv.at[use, o], (k, sp_at(o))))

    def arrive_sp(buffer, use):
        for o in range(1, n_sp):
            src = sp_at(-o)
            remote(buffer.at[src], buffer.at[src], sp_send.at[use, o], sp_recv.at[use, o], (k, src)).wait_recv()

    def to_sides(src, dst, use, cond=None):
        up = has_high if cond is None else jnp.logical_and(has_high, cond)
        down = has_low if cond is None else jnp.logical_and(has_low, cond)
        start(remote(src, dst.at[0], st_send.at[use], st_recv.at[use], (k, sp_at(1))), up)
        start(remote(src, dst.at[1], st_send.at[use + 1], st_recv.at[use + 1], (k, sp_at(-1))), down)

    def from_sides(src, dst, use, cond=None):
        up = has_low if cond is None else jnp.logical_and(has_low, cond)
        down = has_high if cond is None else jnp.logical_and(has_high, cond)
        pl.when(up)(remote(src, dst.at[0], st_send.at[use], st_recv.at[use], (k, sp_at(-1))).wait_recv)
        pl.when(down)(remote(src, dst.at[1], st_send.at[use + 1], st_recv.at[use + 1], (k, sp_at(1))).wait_recv)

    start(remote(iev.at[0], iev_next, st_send.at[0], st_recv.at[0], (tm_at(-1), s)), has_prev)
    to_sides(wind.at[:, 0], wind_ext, 2)
    dec_all[k] = decay[0]
    spread_tm(dec_all, 0)

    blocks = width // 128
    tiles = fields * blocks * rows
    n_obs = obs.shape[1]
    acc = jnp.zeros((6 * tiles, 128), jnp.float32)
    for at in range(0, n_obs, CHUNK):
        part = pl.ds(at, CHUNK)
        cell = obs[:, part]
        wgt = weight[:, part]
        field = cell // (rows * width)
        row = lax.rem(cell // width, rows)
        block = lax.rem(cell // 128, blocks)
        tile = (field * blocks + block) * rows + row
        lane = jnp.bitwise_and(cell, 127)
        left = (lax.broadcasted_iota(jnp.int32, (tiles, CHUNK), 0) == tile).astype(jnp.float32)
        left = left.astype(jnp.bfloat16).reshape(tiles // 16, 16, CHUNK)
        right = (lax.broadcasted_iota(jnp.int32, (128, CHUNK), 0) == lane).astype(jnp.float32).astype(jnp.bfloat16)
        parts = []
        for values in (wgt, wgt * innov[:, part]):
            for piece in split3(jnp.broadcast_to(values, (16, CHUNK))):
                parts.append((left * piece[None]).reshape(tiles, CHUNK))
        acc = acc + lax.dot_general(
            jnp.concatenate(parts, axis=0), right, (((1,), (1,)), ((), ())),
            preferred_element_type=jnp.float32,
        )

    def total(which):
        base = 3 * which * tiles
        x = acc[base : base + tiles] + acc[base + tiles : base + 2 * tiles] + acc[base + 2 * tiles : base + 3 * tiles]
        return jnp.stack([
            jnp.concatenate([x[(f * blocks + b) * rows :][:rows] for b in range(blocks)], axis=1)
            for f in range(fields)
        ])

    diag[...] = total(0)
    r_all[k] = total(1)
    spread_tm(r_all, 1)

    from_sides(wind.at[:, 0], wind_ext, 2)
    pl.when(has_next)(remote(iev.at[0], iev_next, st_send.at[0], st_recv.at[0], (tm_at(1), s)).wait_recv)
    to_sides(iev_next, iev_ext, 4, has_next)
    zero = jnp.zeros((rows, width), jnp.float32)
    flow = [
        jnp.concatenate([
            jnp.where(has_low, wind_ext[0, c], zero), wind[c, 0], jnp.where(has_high, wind_ext[1, c], zero)
        ], axis=0)
        for c in range(2)
    ]
    line = lax.broadcasted_iota(jnp.int32, (3 * rows, width), 0)
    column = lax.broadcasted_iota(jnp.int32, (3 * rows, width), 1)
    inside = jnp.logical_and(line + (s - 1) * rows >= 0, line + (s - 1) * rows < n_sp * rows)
    mask = inside.astype(jnp.float32)
    own = mask * (1.0 - 4.0 * DIFFUSION)
    c_up = mask * (DIFFUSION - 0.5 * flow[0])
    c_down = mask * (DIFFUSION + 0.5 * flow[0])
    c_right = jnp.where(column < width - 1, mask * (DIFFUSION - 0.5 * flow[1]), 0.0)
    c_left = jnp.where(column > 0, mask * (DIFFUSION + 0.5 * flow[1]), 0.0)
    high = 3 * rows - 1

    def model(u):
        for _ in range(STEPS):
            u = (
                own * u + c_up * pltpu.roll(u, high, 0) + c_down * pltpu.roll(u, 1, 0)
                + c_right * pltpu.roll(u, width - 1, 1) + c_left * pltpu.roll(u, 1, 1)
            )
        return u

    def adjoint(v):
        for _ in range(STEPS):
            v = (
                own * v + pltpu.roll(c_up * v, 1, 0) + pltpu.roll(c_down * v, high, 0)
                + pltpu.roll(c_right * v, 1, 1) + pltpu.roll(c_left * v, width - 1, 1)
            )
        return v

    def precondition(source, target):
        for f in range(fields):
            v = [source[j, f] for j in range(n_tm)]
            for j in range(n_tm - 2, -1, -1):
                v[j] = v[j] + dec_all[j, f] * v[j + 1]
            for j in range(1, n_tm):
                v[j] = v[j] + dec_all[j - 1, f] * v[j - 1]
            for j in range(n_tm):
                target[j, f] = v[j]

    def send_pair(source, it):
        to_sides(source.at[pl.ds(k, 2)], d_ext.at[it], 6 + 2 * it)

    def hessian(source, it, first):
        from_sides(source.at[pl.ds(k, 2)], d_ext.at[it], 6 + 2 * it)

        def three(which, f):
            return jnp.concatenate([
                jnp.where(has_low, d_ext[it, 0, which, f], zero), source[k + which, f],
                jnp.where(has_high, d_ext[it, 1, which, f], zero),
            ], axis=0)

        ahead = []
        for f in range(fields):
            ahead.append(model(three(0, f)))
            f_send[it, f] = ahead[f][rows : 2 * rows]
        start(remote(f_send.at[it], f_recv.at[it], st_send.at[10 + it], st_recv.at[10 + it], (tm_at(1), s)), has_next)
        if first:
            from_sides(iev_next, iev_ext, 4, has_next)
        low_ok, high_ok = jnp.logical_and(has_low, has_next), jnp.logical_and(has_high, has_next)
        backs = []
        for f in range(fields):
            inverse = jnp.concatenate([
                jnp.where(low_ok, iev_ext[0, f], zero), jnp.where(has_next, iev_next[f], zero),
                jnp.where(high_ok, iev_ext[1, f], zero),
            ], axis=0)
            backs.append(adjoint(inverse * (three(1, f) - ahead[f]))[rows : 2 * rows])
        pl.when(has_prev)(
            remote(f_send.at[it], f_recv.at[it], st_send.at[10 + it], st_recv.at[10 + it], (tm_at(-1), s)).wait_recv
        )
        image = []
        for f in range(fields):
            p = source[k, f]
            displaced = jnp.where(has_prev, f_recv[it, f], zero)
            image.append(iev[0, f] * (p - displaced) - backs[f] + diag[f] * p)
        return jnp.stack(image)

    z_all[n_tm] = jnp.zeros_like(z_all[n_tm])
    y_all[n_tm] = jnp.zeros_like(y_all[n_tm])
    arrive_tm(dec_all, 0)
    arrive_tm(r_all, 1)
    precondition(r_all, z_all)
    send_pair(z_all, 0)
    q = hessian(z_all, 0, True)
    z = z_all[k]
    r = r_all[k]
    sum_tm[0, k, 0] = folded(r * z)
    sum_tm[0, k, 1] = folded(z * q)
    q_all[k] = q
    spread_tm(sum_tm.at[0], 3)
    spread_tm(q_all, 2)
    arrive_tm(sum_tm.at[0], 3)
    sum_sp[0, s] = jnp.sum(sum_tm[0], axis=0)
    spread_sp(sum_sp.at[0], 0)
    arrive_tm(q_all, 2)
    precondition(q_all, y_all)
    send_pair(y_all, 1)
    w = hessian(y_all, 1, False)
    arrive_sp(sum_sp.at[0], 0)
    sums = jnp.sum(sum_sp[0], axis=0)
    rz, dq = whole(sums[0]), whole(sums[1])
    alpha = rz / dq
    z = z_all[k]
    r = r_all[k]
    q = q_all[k]
    r2 = r - alpha * q
    z2 = z - alpha * y_all[k]
    az2 = q - alpha * w
    sum_tm[1, k, 0] = folded(r2 * z2)
    sum_tm[1, k, 1] = folded(z2 * az2)
    sum_tm[1, k, 2] = folded(z2 * q + z * az2)
    spread_tm(sum_tm.at[1], 4)
    arrive_tm(sum_tm.at[1], 4)
    sum_sp[1, s] = jnp.sum(sum_tm[1], axis=0)
    spread_sp(sum_sp.at[1], 1)
    arrive_sp(sum_sp.at[1], 1)
    sums = jnp.sum(sum_sp[1], axis=0)
    rz2 = whole(sums[0])
    beta = rz2 / rz
    alpha2 = rz2 / (whole(sums[1]) + beta * whole(sums[2]) + beta * beta * dq)
    inc_out[0] = alpha * z + alpha2 * (z2 + beta * z)
    res_out[0] = r2 - alpha2 * (az2 + beta * q)
    for copy, cond in pending:
        if cond is None:
            copy.wait_send()
        else:
            pl.when(cond)(copy.wait_send)


def on_device(wind, decay, iev, obs, weight, innov):
    n_tm, n_sp = lax.axis_size("tm"), lax.axis_size("space")
    tile = decay.shape[1:]
    f32 = jnp.float32
    vmem = pl.BlockSpec(memory_space=pltpu.VMEM)
    field = jax.ShapeDtypeStruct(decay.shape, f32)
    return pl.pallas_call(
        functools.partial(kernel, n_tm, n_sp),
        out_shape=(field, field),
        in_specs=[vmem] * 6,
        out_specs=(vmem, vmem),
        scratch_shapes=[
            pltpu.VMEM((n_tm,) + tile, f32),
            pltpu.VMEM((n_tm,) + tile, f32),
            pltpu.VMEM((n_tm,) + tile, f32),
            pltpu.VMEM((n_tm + 1,) + tile, f32),
            pltpu.VMEM((n_tm + 1,) + tile, f32),
            pltpu.VMEM((2, 2) + tile[1:], f32),
            pltpu.VMEM(tile, f32),
            pltpu.VMEM((2,) + tile, f32),
            pltpu.VMEM((2, 2, 2) + tile, f32),
            pltpu.VMEM((2,) + tile, f32),
            pltpu.VMEM((2,) + tile, f32),
            pltpu.VMEM((2, n_tm, 3, 8, 128), f32),
            pltpu.VMEM((2, n_sp, 3, 8, 128), f32),
            pltpu.VMEM(tile, f32),
            pltpu.SemaphoreType.DMA((5, n_tm)),
            pltpu.SemaphoreType.DMA((5, n_tm)),
            pltpu.SemaphoreType.DMA((2, n_sp)),
            pltpu.SemaphoreType.DMA((2, n_sp)),
            pltpu.SemaphoreType.DMA((12,)),
            pltpu.SemaphoreType.DMA((12,)),
        ],
        compiler_params=pltpu.CompilerParams(
            collective_id=0, has_side_effects=True, vmem_limit_bytes=48 * 1024 * 1024
        ),
    )(wind, decay, iev, obs, weight, innov)


def solution(mesh):
    placed = (
        P(None, "tm", "space", None),
        P("tm", None, "space", None),
        P("tm", None, "space", None),
        P("tm", "space"),
        P("tm", "space"),
        P("tm", "space"),
    )
    return jax.shard_map(
        on_device,
        mesh=mesh,
        in_specs=placed,
        out_specs=(P("tm", None, "space", None), P("tm", None, "space", None)),
        check_vma=False,
    )
```

time: 461 us -> 51.3 us (0.11)
  blocking collectives: 200 us -> 0 us
  starting transfers between devices: 100 us -> 0 us
  other arithmetic: 72.1 us -> 0 us
  Pallas kernels: 0 us -> 44.4 us
  local copies, waits for them, and re-layouts: 48.9 us -> 5.74 us
  waiting for transfers between devices: 31.9 us -> 0 us
  between operations: 5.55 us -> 0.65 us
    psum x3 -> x0, blocking collectives: 130 us -> none  [the longest x2 85 us: inner_product(): return lax.psum(jnp.sum(residual * precond), ('tm', 'space'))]
    ppermute x36 -> x0, starting transfers between devices: 100 us -> none  [the longest x16 69.7 us: with_halo(): lax.ppermute(lax.slice_in_dim(block, block.shape[dim] - width, None, axis...]
    all_gather x5 -> x0, blocking collectives: 70.5 us -> none  [carried_in(): everything = jax.tree.map(lambda part: lax.all_gather(part, axis), shard)]
    scatter-add x3 -> x0, other arithmetic: 65.7 us -> none  [scatter_obs(): return jax.ops.segment_sum(values, index, num_segments=cells).reshape(shape)]
    gather x2 -> x0, local copies, waits for them, and re-layouts: 46.1 us -> none  [on_device(): picked = direction.reshape(cells)[index]]
    pallas_call x0 -> x1, Pallas kernels: none -> 44.4 us  [on_device(): pl.pallas_call(functools.partial(kernel, n_tm, n_sp), out_shape=(field, f...]
    ppermute x36 -> x0, waiting for transfers between devices: 31.9 us -> none  [the longest x16 23.3 us: with_halo(): lax.ppermute(lax.slice_in_dim(block, 0, width, axis=dim), axis, backward)]
    unnamed x12 -> x14, local copies, waits for them, and re-layouts: 0.79 us -> 5.74 us
  transfers between devices with their start and end apart: 36 -> 0, of which waited for: 17 -> 0; matrix products, arithmetic and copies ran while one was open for 20% -> 0% of each run, Pallas kernels for 0% -> 0%
where the time goes in v1:
time: 51.3 us; the launch traced here: 50.8 us
  Pallas kernels  44.4 us (87%)
  local copies, waits for them, and re-layouts  5.74 us (11%)
  between operations  0.65 us (1%)
    pallas_call x1, Pallas kernels, on_device(): pl.pallas_call(functools.partial(kernel, n_tm, n_sp), out_shape=(field, f...  44.4 us
    unnamed x14, local copies, waits for them, and re-layouts  5.74 us

profile of v1, /device:TPU:0, one launch (start us, length us, event | category | flops | bytes accessed | tf_op | source)
XLA Modules:
  0.0 50.8 jit_solution(13952312975602195426)
XLA Ops:
  0.6 0.0 copy-start
  0.6 0.8 %copy-done = f32[1,3,8,512]{3,2,1,0:T(8,128)S(1)} copy-done((f32[1,3,8,512]{3,2,1,0:T(8,128)S(1)}, f32[1,3,8,512]{3,2,1,0:T(8,128)}, u32[]{:S(2)}) %copy-start) | copy-done | bytes 49176
  1.4 0.0 copy-start.1
  1.4 0.8 %copy-done.1 = f32[1,3,8,512]{3,2,1,0:T(8,128)S(1)} copy-done((f32[1,3,8,512]{3,2,1,0:T(8,128)S(1)}, f32[1,3,8,512]{3,2,1,0:T(8,128)}, u32[]{:S(2)}) %copy-start.1) | copy-done | bytes 49176
  2.2 0.0 copy-start.2
  2.2 0.8 %copy-done.2 = f32[2,1,8,512]{3,2,1,0:T(8,128)S(1)} copy-done((f32[2,1,8,512]{3,2,1,0:T(8,128)S(1)}, f32[2,1,8,512]{3,2,1,0:T(8,128)}, u32[]{:S(2)}) %copy-start.2) | copy-done | bytes 32792
  3.0 0.0 copy-start.3
  3.0 0.7 %copy-done.3 = s32[1,4096]{1,0:T(1,128)S(1)} copy-done((s32[1,4096]{1,0:T(1,128)S(1)}, s32[1,4096]{1,0:T(1,128)}, u32[]{:S(2)}) %copy-start.3) | copy-done | bytes 16408
  3.7 0.0 copy-start.4
  3.7 0.7 %copy-done.4 = f32[1,4096]{1,0:T(1,128)S(1)} copy-done((f32[1,4096]{1,0:T(1,128)S(1)}, f32[1,4096]{1,0:T(1,128)}, u32[]{:S(2)}) %copy-start.4) | copy-done | bytes 16408
  4.4 0.0 copy-start.5
  4.4 0.7 %copy-done.5 = f32[1,4096]{1,0:T(1,128)S(1)} copy-done((f32[1,4096]{1,0:T(1,128)S(1)}, f32[1,4096]{1,0:T(1,128)}, u32[]{:S(2)}) %copy-start.5) | copy-done | bytes 16408
  5.1 44.4 %shard_map.77 = (f32[1,3,8,512]{3,2,1,0:T(8,128)S(1)}, f32[1,3,8,512]{3,2,1,0:T(8,128)S(1)}) custom-call(f32[2,1,8,512]{3,2,1,0:T(8,128)S(1)} %copy-done.2, f32[1,3,8,512]{3,2,1,0:T(8,128)S(1)} %copy-done, f32[1,3,8,512]{3,2,1,0:T(8,128)S(1)} %copy-done.1, s32[1,4096]{1,0:T(1,128)S(1)} %copy-done.3, f32[1,4096]{1,0:T(1,128)S(1)} %copy-done.4, ...), custom_call_target="tpu_custom_call" | custom-call | tf_op jit(solution)/shard_map/pallas_call | solution.py:289
  49.6 0.6 %copy.10 = f32[1,3,8,512]{3,2,1,0:T(8,128)} copy(f32[1,3,8,512]{3,2,1,0:T(8,128)S(1)} %get-tuple-element.4) | data formatting | bytes 98304
  50.2 0.6 %copy.11 = f32[1,3,8,512]{3,2,1,0:T(8,128)} copy(f32[1,3,8,512]{3,2,1,0:T(8,128)S(1)} %get-tuple-element.5) | data formatting | bytes 98304
Async XLA Ops:
  0.6 0.8 %copy-start = (f32[1,3,8,512]{3,2,1,0:T(8,128)S(1)}, f32[1,3,8,512]{3,2,1,0:T(8,128)}, u32[]{:S(2)}) copy-start(f32[1,3,8,512]{3,2,1,0:T(8,128)} %decay.1) | copy-start | bytes 147460
  1.4 0.8 %copy-start.1 = (f32[1,3,8,512]{3,2,1,0:T(8,128)S(1)}, f32[1,3,8,512]{3,2,1,0:T(8,128)}, u32[]{:S(2)}) copy-start(f32[1,3,8,512]{3,2,1,0:T(8,128)} %iev.1) | copy-start | bytes 147460
  2.2 0.8 %copy-start.2 = (f32[2,1,8,512]{3,2,1,0:T(8,128)S(1)}, f32[2,1,8,512]{3,2,1,0:T(8,128)}, u32[]{:S(2)}) copy-start(f32[2,1,8,512]{3,2,1,0:T(8,128)} %wind.1) | copy-start | bytes 98308
  3.0 0.7 %copy-start.3 = (s32[1,4096]{1,0:T(1,128)S(1)}, s32[1,4096]{1,0:T(1,128)}, u32[]{:S(2)}) copy-start(s32[1,4096]{1,0:T(1,128)} %obs.1) | copy-start | bytes 49156
  3.7 0.7 %copy-start.4 = (f32[1,4096]{1,0:T(1,128)S(1)}, f32[1,4096]{1,0:T(1,128)}, u32[]{:S(2)}) copy-start(f32[1,4096]{1,0:T(1,128)} %weight.1) | copy-start | bytes 49156
  4.4 0.7 %copy-start.5 = (f32[1,4096]{1,0:T(1,128)S(1)}, f32[1,4096]{1,0:T(1,128)}, u32[]{:S(2)}) copy-start(f32[1,4096]{1,0:T(1,128)} %innov.1) | copy-start | bytes 49156

commit v2 on v1

v2 whole, which is shorter than its diff:
```python
import functools

import jax
import jax.numpy as jnp
from jax import lax
from jax.experimental import pallas as pl
from jax.experimental.pallas import tpu as pltpu
from jax.sharding import PartitionSpec as P

STEPS = 4
DIFFUSION = 0.15
MESH = pl.DeviceIdType.MESH
CHUNK = 1024


def split3(x):
    high = x.astype(jnp.bfloat16)
    rest = x - high.astype(jnp.float32)
    mid = rest.astype(jnp.bfloat16)
    low = (rest - mid.astype(jnp.float32)).astype(jnp.bfloat16)
    return high, mid, low


def folded(x):
    total = x[:, :128]
    for at in range(128, x.shape[1], 128):
        total = total + x[:, at : at + 128]
    return total


def packed(*terms):
    line = lax.broadcasted_iota(jnp.int32, (8, 128), 0)
    out = jnp.zeros((8, 128), jnp.float32)
    for at, term in enumerate(terms):
        out = jnp.where(line == at, jnp.sum(term, axis=0, keepdims=True), out)
    return out


def whole(x, at):
    return jnp.sum(x[at : at + 1], axis=1, keepdims=True)


def kernel(
    n_tm, n_sp, wind_in, decay_in, iev_in, obs_in, weight_in, innov_in, out,
    wind, decay, iev, obs, weight, innov, load_sem, dec_all, r_all, q_all, z_all, y_all, wind_ext, wind_prev, wind_prev_ext, iev_next, iev_ext, d_ext, pack,
    sum_tm, sum_sp, diag, tm_send, tm_recv, sp_send, sp_recv, st_send, st_recv,
):
    k = lax.axis_index("tm")
    s = lax.axis_index("space")
    fields, rows, width = decay_in.shape[1:]
    has_next, has_prev = k < n_tm - 1, k > 0
    has_high, has_low = s < n_sp - 1, s > 0
    pending = []

    def tm_at(o):
        return lax.rem(k + o + n_tm, n_tm)

    def sp_at(o):
        return lax.rem(s + o + n_sp, n_sp)

    loads = [
        pltpu.make_async_copy(src, dst, load_sem.at[at])
        for at, (src, dst) in enumerate((
            (obs_in, obs), (weight_in, weight), (innov_in, innov),
            (decay_in, decay), (iev_in, iev), (wind_in, wind),
        ))
    ]
    for load in loads:
        load.start()
    barrier = pltpu.get_barrier_semaphore()
    for o in range(1, n_tm):
        pl.semaphore_signal(barrier, inc=1, device_id=(tm_at(o), s), device_id_type=MESH)
    for o in range(1, n_sp):
        pl.semaphore_signal(barrier, inc=1, device_id=(k, sp_at(o)), device_id_type=MESH)
    pl.semaphore_wait(barrier, n_tm + n_sp - 2)

    def remote(src, dst, send, recv, device):
        return pltpu.make_async_remote_copy(
            src_ref=src, dst_ref=dst, send_sem=send, recv_sem=recv,
            device_id=device, device_id_type=MESH,
        )

    def start(copy, cond=None):
        pending.append((copy, cond))
        if cond is None:
            copy.start()
        else:
            pl.when(cond)(copy.start)

    def spread_tm(pick, use, f=0):
        for o in range(1, n_tm):
            start(remote(pick(k), pick(k), tm_send.at[use, f, o], tm_recv.at[use, f, o], (tm_at(o), s)))

    def arrive_tm(pick, use, f=0):
        for o in range(1, n_tm):
            src = tm_at(-o)
            remote(pick(src), pick(src), tm_send.at[use, f, o], tm_recv.at[use, f, o], (src, s)).wait_recv()

    def spread_sp(buffer, use):
        for o in range(1, n_sp):
            start(remote(buffer.at[s], buffer.at[s], sp_send.at[use, o], sp_recv.at[use, o], (k, sp_at(o))))

    def arrive_sp(buffer, use):
        for o in range(1, n_sp):
            src = sp_at(-o)
            remote(buffer.at[src], buffer.at[src], sp_send.at[use, o], sp_recv.at[use, o], (k, src)).wait_recv()

    def both(first, second):
        return first if second is None else jnp.logical_and(first, second)

    def to_sides(up, down, low, high, use, cond=None):
        start(remote(up, low, st_send.at[use], st_recv.at[use], (k, sp_at(1))), both(has_high, cond))
        start(remote(down, high, st_send.at[use + 1], st_recv.at[use + 1], (k, sp_at(-1))), both(has_low, cond))

    def from_sides(up, down, low, high, use, cond=None):
        pl.when(both(has_low, cond))(
            remote(up, low, st_send.at[use], st_recv.at[use], (k, sp_at(-1))).wait_recv)
        pl.when(both(has_high, cond))(
            remote(down, high, st_send.at[use + 1], st_recv.at[use + 1], (k, sp_at(1))).wait_recv)

    winds = (wind.at[:, 0], wind.at[:, 0], wind_ext.at[0], wind_ext.at[1], 2)
    ievs = (iev_next, iev_next, iev_ext.at[0], iev_ext.at[1], 4, has_next)
    prevs = (wind_prev, wind_prev, wind_prev_ext.at[0], wind_prev_ext.at[1], 6, has_prev)

    for load in loads:
        load.wait()

    start(remote(iev.at[0], iev_next, st_send.at[0], st_recv.at[0], (tm_at(-1), s)), has_prev)
    start(remote(wind.at[:, 0], wind_prev, st_send.at[1], st_recv.at[1], (tm_at(1), s)), has_next)
    to_sides(*winds)
    dec_all[k] = decay[0]
    for f in range(fields):
        spread_tm(lambda j: dec_all.at[j, f], 0, f)

    blocks = width // 128
    tiles = fields * blocks * rows
    n_obs = obs.shape[1]
    acc = jnp.zeros((6 * tiles, 128), jnp.float32)
    for at in range(0, n_obs, CHUNK):
        part = pl.ds(at, CHUNK)
        cell = obs[:, part]
        wgt = weight[:, part]
        field = cell // (rows * width)
        row = lax.rem(cell // width, rows)
        block = lax.rem(cell // 128, blocks)
        tile = (field * blocks + block) * rows + row
        lane = jnp.bitwise_and(cell, 127)
        left = (lax.broadcasted_iota(jnp.int32, (tiles, CHUNK), 0) == tile).astype(jnp.float32)
        left = left.astype(jnp.bfloat16).reshape(tiles // 16, 16, CHUNK)
        right = (lax.broadcasted_iota(jnp.int32, (128, CHUNK), 0) == lane).astype(jnp.float32).astype(jnp.bfloat16)
        parts = []
        for values in (wgt, wgt * innov[:, part]):
            for piece in split3(jnp.broadcast_to(values, (16, CHUNK))):
                parts.append((left * piece[None]).reshape(tiles, CHUNK))
        acc = acc + lax.dot_general(
            jnp.concatenate(parts, axis=0), right, (((1,), (1,)), ((), ())),
            preferred_element_type=jnp.float32,
        )

    def total(which):
        base = 3 * which * tiles
        x = acc[base : base + tiles] + acc[base + tiles : base + 2 * tiles] + acc[base + 2 * tiles : base + 3 * tiles]
        return jnp.stack([
            jnp.concatenate([x[(f * blocks + b) * rows :][:rows] for b in range(blocks)], axis=1)
            for f in range(fields)
        ])

    r_all[k] = total(1)
    for f in range(fields):
        spread_tm(lambda j: r_all.at[j, f], 1, f)
    diag[...] = total(0)

    pl.when(has_next)(remote(iev.at[0], iev_next, st_send.at[0], st_recv.at[0], (tm_at(1), s)).wait_recv)
    to_sides(*ievs)
    pl.when(has_prev)(remote(wind.at[:, 0], wind_prev, st_send.at[1], st_recv.at[1], (tm_at(-1), s)).wait_recv)
    to_sides(*prevs)
    zero = jnp.zeros((rows, width), jnp.float32)
    high = 3 * rows - 1
    half = rows // 2
    top = lax.broadcasted_iota(jnp.int32, (rows, width), 0) < half

    def three(low, mid, upper):
        return jnp.concatenate([jnp.where(has_low, low, zero), mid, jnp.where(has_high, upper, zero)], axis=0)

    def coefficients(flow):
        line = lax.broadcasted_iota(jnp.int32, (3 * rows, width), 0)
        column = lax.broadcasted_iota(jnp.int32, (3 * rows, width), 1)
        inside = jnp.logical_and(line + (s - 1) * rows >= 0, line + (s - 1) * rows < n_sp * rows)
        mask = inside.astype(jnp.float32)
        return (
            mask * (1.0 - 4.0 * DIFFUSION),
            mask * (DIFFUSION - 0.5 * flow[0]),
            mask * (DIFFUSION + 0.5 * flow[0]),
            jnp.where(column < width - 1, mask * (DIFFUSION - 0.5 * flow[1]), 0.0),
            jnp.where(column > 0, mask * (DIFFUSION + 0.5 * flow[1]), 0.0),
        )

    def model(u, by):
        own, c_up, c_down, c_right, c_left = by
        for _ in range(STEPS):
            u = (
                own * u + c_up * pltpu.roll(u, high, 0) + c_down * pltpu.roll(u, 1, 0)
                + c_right * pltpu.roll(u, width - 1, 1) + c_left * pltpu.roll(u, 1, 1)
            )
        return u

    def adjoint(v, by):
        own, c_up, c_down, c_right, c_left = by
        for _ in range(STEPS):
            v = (
                own * v + pltpu.roll(c_up * v, 1, 0) + pltpu.roll(c_down * v, high, 0)
                + pltpu.roll(c_right * v, 1, 1) + pltpu.roll(c_left * v, width - 1, 1)
            )
        return v

    def precondition(source, target, f):
        v = [source[j, f] for j in range(n_tm)]
        for j in range(n_tm - 2, -1, -1):
            v[j] = v[j] + dec_all[j, f] * v[j + 1]
        for j in range(1, n_tm):
            v[j] = v[j] + dec_all[j - 1, f] * v[j - 1]
        for j in range(n_tm):
            target[j + 1, f] = v[j]

    def pairs(it, f):
        return (pack.at[it, 0, f], pack.at[it, 1, f], d_ext.at[it, 0, f], d_ext.at[it, 1, f], 8 + 2 * (fields * it + f))

    def send_pair(source, it, f):
        before, here, after = pltpu.roll(source[k, f], half, 0), source[k + 1, f], source[k + 2, f]
        pack[it, 0, f, 0] = here
        pack[it, 1, f, 0] = here
        pack[it, 0, f, 1] = jnp.where(top, before, after)
        pack[it, 1, f, 1] = jnp.where(top, after, before)
        to_sides(*pairs(it, f))

    def hessian(source, it, f):
        from_sides(*pairs(it, f))
        p = source[k + 1, f]
        low, upper = d_ext[it, 0, f, 1], d_ext[it, 1, f, 1]
        ahead = model(three(d_ext[it, 0, f, 0], p, d_ext[it, 1, f, 0]), by_here)
        inverse = jnp.where(has_next, three(iev_ext[0, f], iev_next[f], iev_ext[1, f]), 0.0)
        back = adjoint(inverse * (three(low, source[k + 2, f], upper) - ahead), by_here)[rows : 2 * rows]
        before = three(pltpu.roll(low, half, 0), source[k, f], pltpu.roll(upper, half, 0))
        displaced = model(before, by_prev)[rows : 2 * rows]
        return iev[0, f] * (p - displaced) - back + diag[f] * p

    for edge in (0, n_tm + 1):
        z_all[edge] = jnp.zeros_like(z_all[edge])
        y_all[edge] = jnp.zeros_like(y_all[edge])
    from_sides(*winds)
    by_here = coefficients([three(wind_ext[0, c], wind[c, 0], wind_ext[1, c]) for c in range(2)])
    for f in range(fields):
        arrive_tm(lambda j: dec_all.at[j, f], 0, f)
        arrive_tm(lambda j: r_all.at[j, f], 1, f)
        precondition(r_all, z_all, f)
        send_pair(z_all, 0, f)
    from_sides(*ievs)
    from_sides(*prevs)
    by_prev = coefficients([
        jnp.where(has_prev, three(wind_prev_ext[0, c], wind_prev[c], wind_prev_ext[1, c]), 0.0) for c in range(2)
    ])
    rz_part = dq_part = 0.0
    for f in range(fields):
        q = hessian(z_all, 0, f)
        q_all[k, f] = q
        spread_tm(lambda j: q_all.at[j, f], 2, f)
        z = z_all[k + 1, f]
        rz_part = rz_part + folded(r_all[k, f] * z)
        dq_part = dq_part + folded(z * q)
    sum_tm[0, k] = packed(rz_part, dq_part)
    spread_tm(lambda j: sum_tm.at[0, j], 3)
    for f in range(fields):
        arrive_tm(lambda j: q_all.at[j, f], 2, f)
        precondition(q_all, y_all, f)
        send_pair(y_all, 1, f)
    arrive_tm(lambda j: sum_tm.at[0, j], 3)
    sum_sp[0, s] = jnp.sum(sum_tm[0], axis=0)
    spread_sp(sum_sp.at[0], 0)
    w = [hessian(y_all, 1, f) for f in range(fields)]
    arrive_sp(sum_sp.at[0], 0)
    sums = jnp.sum(sum_sp[0], axis=0)
    rz, dq = whole(sums, 0), whole(sums, 1)
    alpha = rz / dq
    parts = [0.0, 0.0, 0.0]
    held = []
    for f in range(fields):
        z, q = z_all[k + 1, f], q_all[k, f]
        r2 = r_all[k, f] - alpha * q
        z2 = z - alpha * y_all[k + 1, f]
        az2 = q - alpha * w[f]
        parts[0] = parts[0] + folded(r2 * z2)
        parts[1] = parts[1] + folded(z2 * az2)
        parts[2] = parts[2] + folded(z2 * q + z * az2)
        held.append((r2, z2, az2))
    sum_tm[1, k] = packed(*parts)
    spread_tm(lambda j: sum_tm.at[1, j], 4)
    arrive_tm(lambda j: sum_tm.at[1, j], 4)
    sum_sp[1, s] = jnp.sum(sum_tm[1], axis=0)
    spread_sp(sum_sp.at[1], 1)
    arrive_sp(sum_sp.at[1], 1)
    sums = jnp.sum(sum_sp[1], axis=0)
    rz2 = whole(sums, 0)
    beta = rz2 / rz
    alpha2 = rz2 / (whole(sums, 1) + beta * whole(sums, 2) + beta * beta * dq)
    for f in range(fields):
        r2, z2, az2 = held[f]
        z, q = z_all[k + 1, f], q_all[k, f]
        out[0, 0, f] = alpha * z + alpha2 * (z2 + beta * z)
        out[1, 0, f] = r2 - alpha2 * (az2 + beta * q)
    for copy, cond in pending:
        if cond is None:
            copy.wait_send()
        else:
            pl.when(cond)(copy.wait_send)


def on_device(wind, decay, iev, obs, weight, innov):
    n_tm, n_sp = lax.axis_size("tm"), lax.axis_size("space")
    tile = decay.shape[1:]
    f32 = jnp.float32
    vmem = pl.BlockSpec(memory_space=pltpu.VMEM)
    both = pl.pallas_call(
        functools.partial(kernel, n_tm, n_sp),
        out_shape=jax.ShapeDtypeStruct((2,) + decay.shape, f32),
        in_specs=[pl.BlockSpec(memory_space=pltpu.HBM)] * 6,
        out_specs=vmem,
        scratch_shapes=[
            pltpu.VMEM(wind.shape, f32),
            pltpu.VMEM(decay.shape, f32),
            pltpu.VMEM(iev.shape, f32),
            pltpu.VMEM(obs.shape, jnp.int32),
            pltpu.VMEM(weight.shape, f32),
            pltpu.VMEM(innov.shape, f32),
            pltpu.SemaphoreType.DMA((6,)),
            pltpu.VMEM((n_tm,) + tile, f32),
            pltpu.VMEM((n_tm,) + tile, f32),
            pltpu.VMEM((n_tm,) + tile, f32),
            pltpu.VMEM((n_tm + 2,) + tile, f32),
            pltpu.VMEM((n_tm + 2,) + tile, f32),
            pltpu.VMEM((2, 2) + tile[1:], f32),
            pltpu.VMEM((2,) + tile[1:], f32),
            pltpu.VMEM((2, 2) + tile[1:], f32),
            pltpu.VMEM(tile, f32),
            pltpu.VMEM((2,) + tile, f32),
            pltpu.VMEM((2, 2, tile[0], 2) + tile[1:], f32),
            pltpu.VMEM((2, 2, tile[0], 2) + tile[1:], f32),
            pltpu.VMEM((2, n_tm, 8, 128), f32),
            pltpu.VMEM((2, n_sp, 8, 128), f32),
            pltpu.VMEM(tile, f32),
            pltpu.SemaphoreType.DMA((5, 3, n_tm)),
            pltpu.SemaphoreType.DMA((5, 3, n_tm)),
            pltpu.SemaphoreType.DMA((2, n_sp)),
            pltpu.SemaphoreType.DMA((2, n_sp)),
            pltpu.SemaphoreType.DMA((20,)),
            pltpu.SemaphoreType.DMA((20,)),
        ],
        compiler_params=pltpu.CompilerParams(
            collective_id=0, has_side_effects=True, vmem_limit_bytes=62 * 1024 * 1024
        ),
    )(wind, decay, iev, obs, weight, innov)
    return both[0], both[1]


def solution(mesh):
    placed = (
        P(None, "tm", "space", None),
        P("tm", None, "space", None),
        P("tm", None, "space", None),
        P("tm", "space"),
        P("tm", "space"),
        P("tm", "space"),
    )
    return jax.shard_map(
        on_device,
        mesh=mesh,
        in_specs=placed,
        out_specs=(P("tm", None, "space", None), P("tm", None, "space", None)),
        check_vma=False,
    )
```

time: 51.3 us -> 40.1 us (0.78)
  Pallas kernels: 44.4 us -> 37.8 us
  local copies, waits for them, and re-layouts: 5.74 us -> 1.46 us
    pallas_call x1, Pallas kernels: 44.4 us -> 37.8 us  [on_device(): pl.pallas_call(functools.partial(kernel, n_tm, n_sp), out_shape=jax.Shape...]
    unnamed x14 -> x0, local copies, waits for them, and re-layouts: 5.74 us -> none
    squeeze x0 -> x1, local copies, waits for them, and re-layouts: none -> 1.46 us  [on_device(): return (both[0], both[1])]
where the time goes in v2:
time: 40.1 us; the launch traced here: 39.9 us
  Pallas kernels  37.8 us (94%)
  local copies, waits for them, and re-layouts  1.46 us (4%)
  between operations  0.64 us (2%)
    pallas_call x1, Pallas kernels, on_device(): pl.pallas_call(functools.partial(kernel, n_tm, n_sp), out_shape=jax.Shape...  37.8 us
    squeeze x1, local copies, waits for them, and re-layouts, on_device(): return (both[0], both[1])  1.46 us

profile of v2, /device:TPU:0, one launch (start us, length us, event | category | flops | bytes accessed | tf_op | source)
XLA Modules:
  0.0 39.9 jit_solution(10892698328205688452)
XLA Ops:
  0.6 37.8 %shard_map.77 = f32[2,1,3,8,512]{4,3,2,1,0:T(8,128)} custom-call(f32[2,1,8,512]{3,2,1,0:T(8,128)} %wind_in.1, f32[1,3,8,512]{3,2,1,0:T(8,128)} %decay_in.1, f32[1,3,8,512]{3,2,1,0:T(8,128)} %iev_in.1, s32[1,4096]{1,0:T(1,128)} %obs_in.1, f32[1,4096]{1,0:T(1,128)} %weight_in.1, f32[1,4096]{1,0:T(1,128)} %innov_in.1), custom_call_target="tpu_custom_call" | custom-call | tf_op jit(solution)/shard_map/pallas_call | solution.py:322
  38.4 1.5 %slice_bitcast_fusion = (f32[1,3,8,512]{3,2,1,0:T(8,128)}, f32[1,3,8,512]{3,2,1,0:T(8,128)}) fusion(f32[2,1,3,8,512]{4,3,2,1,0:T(8,128)} %shard_map.77), kind=kLoop, calls=%fused_computation | loop fusion | bytes 196608 | tf_op jit(solution)/shard_map/squeeze | solution.py:361

commit v3 on v2

--- a/solution.py
+++ b/solution.py
@@ -11,6 +11,7 @@
 DIFFUSION = 0.15
 MESH = pl.DeviceIdType.MESH
 CHUNK = 1024
+DIRECT = 64
 
 
 def split3(x):
@@ -43,7 +44,7 @@
 def kernel(
     n_tm, n_sp, wind_in, decay_in, iev_in, obs_in, weight_in, innov_in, out,
     wind, decay, iev, obs, weight, innov, load_sem, dec_all, r_all, q_all, z_all, y_all, wind_ext, wind_prev, wind_prev_ext, iev_next, iev_ext, d_ext, pack,
-    sum_tm, sum_sp, diag, tm_send, tm_recv, sp_send, sp_recv, st_send, st_recv,
+    sum_tm, sum_sp, sum_any, any_send, any_recv, diag, tm_send, tm_recv, sp_send, sp_recv, st_send, st_recv,
 ):
     k = lax.axis_index("tm")
     s = lax.axis_index("space")
@@ -68,11 +69,22 @@
     for load in loads:
         load.start()
     barrier = pltpu.get_barrier_semaphore()
-    for o in range(1, n_tm):
-        pl.semaphore_signal(barrier, inc=1, device_id=(tm_at(o), s), device_id_type=MESH)
-    for o in range(1, n_sp):
-        pl.semaphore_signal(barrier, inc=1, device_id=(k, sp_at(o)), device_id_type=MESH)
-    pl.semaphore_wait(barrier, n_tm + n_sp - 2)
+    me = k * n_sp + s
+    direct = n_tm * n_sp <= DIRECT
+
+    def any_at(o):
+        return lax.rem(me + o + n_tm * n_sp, n_tm * n_sp)
+
+    def place(at):
+        return (at // n_sp, lax.rem(at, n_sp))
+
+    if direct:
+        partners = [place(any_at(o)) for o in range(1, n_tm * n_sp)]
+    else:
+        partners = [(tm_at(o), s) for o in range(1, n_tm)] + [(k, sp_at(o)) for o in range(1, n_sp)]
+    for partner in partners:
+        pl.semaphore_signal(barrier, inc=1, device_id=partner, device_id_type=MESH)
+    pl.semaphore_wait(barrier, len(partners))
 
     def remote(src, dst, send, recv, device):
         return pltpu.make_async_remote_copy(
@@ -129,7 +141,7 @@
     start(remote(wind.at[:, 0], wind_prev, st_send.at[1], st_recv.at[1], (tm_at(1), s)), has_next)
     to_sides(*winds)
     dec_all[k] = decay[0]
-    for f in range(fields):
+    for f in range(2):
         spread_tm(lambda j: dec_all.at[j, f], 0, f)
 
     blocks = width // 128
@@ -168,6 +180,8 @@
     r_all[k] = total(1)
     for f in range(fields):
         spread_tm(lambda j: r_all.at[j, f], 1, f)
+        if f + 2 < fields:
+            spread_tm(lambda j: dec_all.at[j, f + 2], 0, f + 2)
     diag[...] = total(0)
 
     pl.when(has_next)(remote(iev.at[0], iev_next, st_send.at[0], st_recv.at[0], (tm_at(1), s)).wait_recv)
@@ -237,12 +251,16 @@
         from_sides(*pairs(it, f))
         p = source[k + 1, f]
         low, upper = d_ext[it, 0, f, 1], d_ext[it, 1, f, 1]
-        ahead = model(three(d_ext[it, 0, f, 0], p, d_ext[it, 1, f, 0]), by_here)
-        inverse = jnp.where(has_next, three(iev_ext[0, f], iev_next[f], iev_ext[1, f]), 0.0)
-        back = adjoint(inverse * (three(low, source[k + 2, f], upper) - ahead), by_here)[rows : 2 * rows]
         before = three(pltpu.roll(low, half, 0), source[k, f], pltpu.roll(upper, half, 0))
-        displaced = model(before, by_prev)[rows : 2 * rows]
-        return iev[0, f] * (p - displaced) - back + diag[f] * p
+        jump = p - model(before, by_prev)[rows : 2 * rows]
+
+        def close():
+            ahead = model(three(d_ext[it, 0, f, 0], p, d_ext[it, 1, f, 0]), by_here)
+            inverse = jnp.where(has_next, three(iev_ext[0, f], iev_next[f], iev_ext[1, f]), 0.0)
+            back = adjoint(inverse * (three(low, source[k + 2, f], upper) - ahead), by_here)[rows : 2 * rows]
+            return iev[0, f] * jump - back + diag[f] * p
+
+        return jump, close
 
     for edge in (0, n_tm + 1):
         z_all[edge] = jnp.zeros_like(z_all[edge])
@@ -259,9 +277,12 @@
     by_prev = coefficients([
         jnp.where(has_prev, three(wind_prev_ext[0, c], wind_prev[c], wind_prev_ext[1, c]), 0.0) for c in range(2)
     ])
+    jumps = []
     rz_part = dq_part = 0.0
     for f in range(fields):
-        q = hessian(z_all, 0, f)
+        jump, close = hessian(z_all, 0, f)
+        jumps.append(jump)
+        q = close()
         q_all[k, f] = q
         spread_tm(lambda j: q_all.at[j, f], 2, f)
         z = z_all[k + 1, f]
@@ -276,7 +297,8 @@
     arrive_tm(lambda j: sum_tm.at[0, j], 3)
     sum_sp[0, s] = jnp.sum(sum_tm[0], axis=0)
     spread_sp(sum_sp.at[0], 0)
-    w = [hessian(y_all, 1, f) for f in range(fields)]
+    opened = [hessian(y_all, 1, f) for f in range(fields)]
+    closes = [close for _, close in opened]
     arrive_sp(sum_sp.at[0], 0)
     sums = jnp.sum(sum_sp[0], axis=0)
     rz, dq = whole(sums, 0), whole(sums, 1)
@@ -287,24 +309,38 @@
         z, q = z_all[k + 1, f], q_all[k, f]
         r2 = r_all[k, f] - alpha * q
         z2 = z - alpha * y_all[k + 1, f]
-        az2 = q - alpha * w[f]
+        jump2 = jumps[f] - alpha * opened[f][0]
+        scaled, seen = iev[0, f] * jump2, diag[f] * z2
         parts[0] = parts[0] + folded(r2 * z2)
-        parts[1] = parts[1] + folded(z2 * az2)
-        parts[2] = parts[2] + folded(z2 * q + z * az2)
-        held.append((r2, z2, az2))
-    sum_tm[1, k] = packed(*parts)
-    spread_tm(lambda j: sum_tm.at[1, j], 4)
-    arrive_tm(lambda j: sum_tm.at[1, j], 4)
-    sum_sp[1, s] = jnp.sum(sum_tm[1], axis=0)
-    spread_sp(sum_sp.at[1], 1)
-    arrive_sp(sum_sp.at[1], 1)
-    sums = jnp.sum(sum_sp[1], axis=0)
+        parts[1] = parts[1] + folded(scaled * jump2 + seen * z2)
+        parts[2] = parts[2] + folded(2.0 * (scaled * jumps[f] + seen * z))
+        held.append((r2, z2))
+    if direct:
+        sum_any[me] = packed(*parts)
+        for o in range(1, n_tm * n_sp):
+            start(remote(sum_any.at[me], sum_any.at[me], any_send.at[o], any_recv.at[o], place(any_at(o))))
+    else:
+        sum_tm[1, k] = packed(*parts)
+        spread_tm(lambda j: sum_tm.at[1, j], 4)
+    w = [close() for close in closes]
+    if direct:
+        for o in range(1, n_tm * n_sp):
+            src = any_at(-o)
+            remote(sum_any.at[src], sum_any.at[src], any_send.at[o], any_recv.at[o], place(src)).wait_recv()
+        sums = jnp.sum(sum_any[...], axis=0)
+    else:
+        arrive_tm(lambda j: sum_tm.at[1, j], 4)
+        sum_sp[1, s] = jnp.sum(sum_tm[1], axis=0)
+        spread_sp(sum_sp.at[1], 1)
+        arrive_sp(sum_sp.at[1], 1)
+        sums = jnp.sum(sum_sp[1], axis=0)
     rz2 = whole(sums, 0)
     beta = rz2 / rz
     alpha2 = rz2 / (whole(sums, 1) + beta * whole(sums, 2) + beta * beta * dq)
     for f in range(fields):
-        r2, z2, az2 = held[f]
+        r2, z2 = held[f]
         z, q = z_all[k + 1, f], q_all[k, f]
+        az2 = q - alpha * w[f]
         out[0, 0, f] = alpha * z + alpha2 * (z2 + beta * z)
         out[1, 0, f] = r2 - alpha2 * (az2 + beta * q)
     for copy, cond in pending:
@@ -346,6 +382,9 @@
             pltpu.VMEM((2, 2, tile[0], 2) + tile[1:], f32),
             pltpu.VMEM((2, n_tm, 8, 128), f32),
             pltpu.VMEM((2, n_sp, 8, 128), f32),
+            pltpu.VMEM((n_tm * n_sp, 8, 128), f32),
+            pltpu.SemaphoreType.DMA((n_tm * n_sp,)),
+            pltpu.SemaphoreType.DMA((n_tm * n_sp,)),
             pltpu.VMEM(tile, f32),
             pltpu.SemaphoreType.DMA((5, 3, n_tm)),
             pltpu.SemaphoreType.DMA((5, 3, n_tm)),

time: 40.1 us -> 39.3 us (0.980)
  Pallas kernels: 37.8 us -> 37 us
    pallas_call x1, Pallas kernels: 37.8 us -> 37 us  [on_device(): pl.pallas_call(functools.partial(kernel, n_tm, n_sp), out_shape=jax.Shape...]
where the time goes in v3:
time: 39.3 us; the launch traced here: 39.1 us
  Pallas kernels  37 us (94%)
  local copies, waits for them, and re-layouts  1.46 us (4%)
  between operations  0.64 us (2%)
    pallas_call x1, Pallas kernels, on_device(): pl.pallas_call(functools.partial(kernel, n_tm, n_sp), out_shape=jax.Shape...  37 us
    squeeze x1, local copies, waits for them, and re-layouts, on_device(): return (both[0], both[1])  1.46 us

profile of v3, /device:TPU:0, one launch (start us, length us, event | category | flops | bytes accessed | tf_op | source)
XLA Modules:
  0.0 39.1 jit_solution(11184347067510231447)
XLA Ops:
  0.6 37.0 %shard_map.77 = f32[2,1,3,8,512]{4,3,2,1,0:T(8,128)} custom-call(f32[2,1,8,512]{3,2,1,0:T(8,128)} %wind_in.1, f32[1,3,8,512]{3,2,1,0:T(8,128)} %decay_in.1, f32[1,3,8,512]{3,2,1,0:T(8,128)} %iev_in.1, s32[1,4096]{1,0:T(1,128)} %obs_in.1, f32[1,4096]{1,0:T(1,128)} %weight_in.1, f32[1,4096]{1,0:T(1,128)} %innov_in.1), custom_call_target="tpu_custom_call" | custom-call | tf_op jit(solution)/shard_map/pallas_call | solution.py:358
  37.6 1.5 %slice_bitcast_fusion = (f32[1,3,8,512]{3,2,1,0:T(8,128)}, f32[1,3,8,512]{3,2,1,0:T(8,128)}) fusion(f32[2,1,3,8,512]{4,3,2,1,0:T(8,128)} %shard_map.77), kind=kLoop, calls=%fused_computation | loop fusion | bytes 196608 | tf_op jit(solution)/shard_map/squeeze | solution.py:400

commit v4 on v3

--- a/solution.py
+++ b/solution.py
@@ -62,8 +62,8 @@
     loads = [
         pltpu.make_async_copy(src, dst, load_sem.at[at])
         for at, (src, dst) in enumerate((
+            (decay_in, decay), (iev_in, iev), (wind_in, wind),
             (obs_in, obs), (weight_in, weight), (innov_in, innov),
-            (decay_in, decay), (iev_in, iev), (wind_in, wind),
         ))
     ]
     for load in loads:
@@ -99,14 +99,18 @@
         else:
             pl.when(cond)(copy.start)
 
-    def spread_tm(pick, use, f=0):
+    def spread_tm(pick, use, f=0, cond=None):
         for o in range(1, n_tm):
-            start(remote(pick(k), pick(k), tm_send.at[use, f, o], tm_recv.at[use, f, o], (tm_at(o), s)))
-
-    def arrive_tm(pick, use, f=0):
+            start(remote(pick(k), pick(k), tm_send.at[use, f, o], tm_recv.at[use, f, o], (tm_at(o), s)), cond)
+
+    def arrive_tm(pick, use, f=0, count=None):
         for o in range(1, n_tm):
             src = tm_at(-o)
-            remote(pick(src), pick(src), tm_send.at[use, f, o], tm_recv.at[use, f, o], (src, s)).wait_recv()
+            wait = remote(pick(src), pick(src), tm_send.at[use, f, o], tm_recv.at[use, f, o], (src, s)).wait_recv
+            if count is None:
+                wait()
+            else:
+                pl.when(src < count)(wait)
 
     def spread_sp(buffer, use):
         for o in range(1, n_sp):
@@ -134,15 +138,15 @@
     ievs = (iev_next, iev_next, iev_ext.at[0], iev_ext.at[1], 4, has_next)
     prevs = (wind_prev, wind_prev, wind_prev_ext.at[0], wind_prev_ext.at[1], 6, has_prev)
 
-    for load in loads:
+    loads[0].wait()
+    dec_all[k] = decay[0]
+    spread_tm(lambda j: dec_all.at[j, 0], 0, 0, has_next)
+    for load in loads[1:]:
         load.wait()
-
     start(remote(iev.at[0], iev_next, st_send.at[0], st_recv.at[0], (tm_at(-1), s)), has_prev)
     start(remote(wind.at[:, 0], wind_prev, st_send.at[1], st_recv.at[1], (tm_at(1), s)), has_next)
+    spread_tm(lambda j: dec_all.at[j, 1], 0, 1, has_next)
     to_sides(*winds)
-    dec_all[k] = decay[0]
-    for f in range(2):
-        spread_tm(lambda j: dec_all.at[j, f], 0, f)
 
     blocks = width // 128
     tiles = fields * blocks * rows
@@ -181,7 +185,7 @@
     for f in range(fields):
         spread_tm(lambda j: r_all.at[j, f], 1, f)
         if f + 2 < fields:
-            spread_tm(lambda j: dec_all.at[j, f + 2], 0, f + 2)
+            spread_tm(lambda j: dec_all.at[j, f + 2], 0, f + 2, has_next)
     diag[...] = total(0)
 
     pl.when(has_next)(remote(iev.at[0], iev_next, st_send.at[0], st_recv.at[0], (tm_at(1), s)).wait_recv)
@@ -268,7 +272,7 @@
     from_sides(*winds)
     by_here = coefficients([three(wind_ext[0, c], wind[c, 0], wind_ext[1, c]) for c in range(2)])
     for f in range(fields):
-        arrive_tm(lambda j: dec_all.at[j, f], 0, f)
+        arrive_tm(lambda j: dec_all.at[j, f], 0, f, n_tm - 1)
         arrive_tm(lambda j: r_all.at[j, f], 1, f)
         precondition(r_all, z_all, f)
         send_pair(z_all, 0, f)

time: 39.3 us -> 37.8 us (0.962)
  Pallas kernels: 37 us -> 35.6 us
    pallas_call x1, Pallas kernels: 37 us -> 35.6 us  [on_device(): pl.pallas_call(functools.partial(kernel, n_tm, n_sp), out_shape=jax.Shape...]
where the time goes in v4:
time: 37.8 us; the launch traced here: 37.7 us
  Pallas kernels  35.6 us (94%)
  local copies, waits for them, and re-layouts  1.46 us (4%)
  between operations  0.64 us (2%)
    pallas_call x1, Pallas kernels, on_device(): pl.pallas_call(functools.partial(kernel, n_tm, n_sp), out_shape=jax.Shape...  35.6 us
    squeeze x1, local copies, waits for them, and re-layouts, on_device(): return (both[0], both[1])  1.46 us

profile of v4, /device:TPU:0, one launch (start us, length us, event | category | flops | bytes accessed | tf_op | source)
XLA Modules:
  0.0 37.7 jit_solution(11308023889866892221)
XLA Ops:
  0.6 35.6 %shard_map.77 = f32[2,1,3,8,512]{4,3,2,1,0:T(8,128)} custom-call(f32[2,1,8,512]{3,2,1,0:T(8,128)} %wind_in.1, f32[1,3,8,512]{3,2,1,0:T(8,128)} %decay_in.1, f32[1,3,8,512]{3,2,1,0:T(8,128)} %iev_in.1, s32[1,4096]{1,0:T(1,128)} %obs_in.1, f32[1,4096]{1,0:T(1,128)} %weight_in.1, f32[1,4096]{1,0:T(1,128)} %innov_in.1), custom_call_target="tpu_custom_call" | custom-call | tf_op jit(solution)/shard_map/pallas_call | solution.py:362
  36.2 1.5 %slice_bitcast_fusion = (f32[1,3,8,512]{3,2,1,0:T(8,128)}, f32[1,3,8,512]{3,2,1,0:T(8,128)}) fusion(f32[2,1,3,8,512]{4,3,2,1,0:T(8,128)} %shard_map.77), kind=kLoop, calls=%fused_computation | loop fusion | bytes 196608 | tf_op jit(solution)/shard_map/squeeze | solution.py:404

commit v5 on v4

--- a/solution.py
+++ b/solution.py
@@ -141,11 +141,11 @@
     loads[0].wait()
     dec_all[k] = decay[0]
     spread_tm(lambda j: dec_all.at[j, 0], 0, 0, has_next)
+    spread_tm(lambda j: dec_all.at[j, 1], 0, 1, has_next)
     for load in loads[1:]:
         load.wait()
     start(remote(iev.at[0], iev_next, st_send.at[0], st_recv.at[0], (tm_at(-1), s)), has_prev)
     start(remote(wind.at[:, 0], wind_prev, st_send.at[1], st_recv.at[1], (tm_at(1), s)), has_next)
-    spread_tm(lambda j: dec_all.at[j, 1], 0, 1, has_next)
     to_sides(*winds)
 
     blocks = width // 128

time: 37.8 us -> 38.1 us (level)
  no operation moved by 1% of the time
where the time goes in v5:
time: 38.1 us; the launch traced here: 37.9 us
  Pallas kernels  35.8 us (94%)
  local copies, waits for them, and re-layouts  1.46 us (4%)
  between operations  0.64 us (2%)
    pallas_call x1, Pallas kernels, on_device(): pl.pallas_call(functools.partial(kernel, n_tm, n_sp), out_shape=jax.Shape...  35.8 us
    squeeze x1, local copies, waits for them, and re-layouts, on_device(): return (both[0], both[1])  1.46 us

profile of v5, /device:TPU:0, one launch (start us, length us, event | category | flops | bytes accessed | tf_op | source)
XLA Modules:
  0.0 37.9 jit_solution(14229192627907361240)
XLA Ops:
  0.6 35.8 %shard_map.77 = f32[2,1,3,8,512]{4,3,2,1,0:T(8,128)} custom-call(f32[2,1,8,512]{3,2,1,0:T(8,128)} %wind_in.1, f32[1,3,8,512]{3,2,1,0:T(8,128)} %decay_in.1, f32[1,3,8,512]{3,2,1,0:T(8,128)} %iev_in.1, s32[1,4096]{1,0:T(1,128)} %obs_in.1, f32[1,4096]{1,0:T(1,128)} %weight_in.1, f32[1,4096]{1,0:T(1,128)} %innov_in.1), custom_call_target="tpu_custom_call" | custom-call | tf_op jit(solution)/shard_map/pallas_call | solution.py:362
  36.4 1.5 %slice_bitcast_fusion = (f32[1,3,8,512]{3,2,1,0:T(8,128)}, f32[1,3,8,512]{3,2,1,0:T(8,128)}) fusion(f32[2,1,3,8,512]{4,3,2,1,0:T(8,128)} %shard_map.77), kind=kLoop, calls=%fused_computation | loop fusion | bytes 196608 | tf_op jit(solution)/shard_map/squeeze | solution.py:404
